TPU v7x, 32 devices: a whole 2x2x4 slice. The times are simulated.
32 devices in a mesh: gx: 8 (over z, y), gy: 4 (over x, core).
Axes of the slice: x: 2, y: 2, z: 4, core: 2. Of those that a mesh axis runs over, the one named last changes fastest.
Arguments:
- fields: float32 [4, 2048, 16, 2048], P(None, 'gx', None, 'gy'), may hold values from -6 to 6
- slope_x: float32 [2048, 2048], P('gx', 'gy'), may hold values from -0.5 to 0.5
- slope_y: float32 [2048, 2048], P('gx', 'gy'), may hold values from -0.5 to 0.5
- fringe_mask: int32 [2048], P('gx'), may hold values 0 or 1
- plane_x: int32 [1], replicated, may hold values from 0 to 2047
- joint_bin: int32 [2048, 16, 2048], P('gx', None, 'gy'), may hold values from 0 to 4095
Outputs:
- tendency: float32 [4, 2048, 16, 2048], P(None, 'gx', None, 'gy')
- histogram: float32 [64, 64], P('gx', 'gy')
All inputs are finite; a program needn't handle non-finite values. No bound on the sum of `fringe_mask` on one device may be relied on, other than what follows from the above.
Results may differ from a plain program's by a relative error of at most 0.0004.
Values sent between devices are 32-bit elements; how exact they have to be, the bound alone decides.
No kernel may reach another device: no remote copies, remote signals or barrier semaphores. Data moves between devices by JAX's collectives and lax.ppermute only.
A program may use at most 384 MiB of HBM per device.

v0:
```python
import math

import jax
import jax.numpy as jnp
from jax import lax
from jax.sharding import PartitionSpec as P

LEVELS = 384
BINS = 64


FRINGE_RATE = 0.5
BUOYANCY = 0.5
SECTION_DT = 0.25


def broadcast(block, axis, owner):
    block = jnp.where(lax.axis_index(axis) == owner, block, jnp.zeros_like(block))
    return lax.psum(block, axis)


def with_halo(block, sides, width):
    for axis, dim in sides:
        count = lax.axis_size(axis)
        forward = [(i, i + 1) for i in range(count - 1)]
        forward.append((count - 1, 0))
        backward = [(target, source) for source, target in forward]
        low = lax.ppermute(
            lax.slice_in_dim(block, block.shape[dim] - width, None, axis=dim), axis, forward
        )
        high = lax.ppermute(lax.slice_in_dim(block, 0, width, axis=dim), axis, backward)
        block = jnp.concatenate([low, block, high], axis=dim)
    return block


def level_derivative(field):
    levels = field.shape[-2]
    upper = jnp.concatenate([field[..., 1:, :], field[..., -1:, :]], axis=-2)
    lower = jnp.concatenate([field[..., :1, :], field[..., :-1, :]], axis=-2)
    position = lax.iota(jnp.int32, levels)
    spacing = jnp.where((position == 0) | (position == levels - 1), 1.0, 2.0).astype(field.dtype)
    return (upper - lower) / spacing[:, None]


def fourier_matrix(count):
    row_index = lax.iota(jnp.int32, count)[:, None]
    col_index = lax.iota(jnp.int32, count)[None, :]
    offset = (row_index - col_index + count // 2) % count - count // 2
    nonzero = jnp.where(offset == 0, 1, offset)
    angle = jnp.pi * nonzero.astype(jnp.float32) / count
    parity = jnp.where(offset % 2 == 0, 1.0, -1.0)
    values = jnp.pi / count * parity * jnp.cos(angle) / jnp.sin(angle)
    return jnp.where(offset == 0, 0.0, values)


def differentiate(pencil):
    matrix = fourier_matrix(pencil.shape[1])
    return jnp.einsum("ij,njc->nic", matrix, pencil, precision=lax.Precision.HIGHEST)


def shards(fields, slope_x, slope_y, fringe_mask, plane_x, joint_bin):
    field_count, local_rows, levels, local_cols = fields.shape
    total_x = local_rows * lax.axis_size("gx")
    total_y = local_cols * lax.axis_size("gy")
    flattened = fields.reshape(field_count, local_rows, levels * local_cols)
    level_pos = (lax.iota(jnp.int32, levels).astype(jnp.float32) + 0.5) / LEVELS
    shape_factor = (1.0 - level_pos)[None, :, None]
    metric_x = -slope_x[:, None, :] * shape_factor
    metric_y = -slope_y[:, None, :] * shape_factor
    level_slope = level_derivative(fields)
    derived = differentiate(
        lax.all_to_all(flattened, "gx", split_axis=2, concat_axis=1, tiled=True)
    )
    stream_slope = lax.all_to_all(derived, "gx", split_axis=1, concat_axis=2, tiled=True).reshape(
        fields.shape
    )
    owner = plane_x[0] // local_rows
    own_row = lax.dynamic_index_in_dim(fields, plane_x[0] % local_rows, 1, keepdims=True)
    plane = broadcast(own_row, "gx", owner)
    mask_float = fringe_mask.astype(jnp.float32)[:, None, None]
    stream_part = -fields[0] * (
        stream_slope + metric_x * level_slope
    ) + FRINGE_RATE * mask_float * (plane - fields)
    padded = with_halo(fields, (("gy", 3),), 2)
    span_slope = (
        8.0 * (padded[..., 3 : local_cols + 3] - padded[..., 1 : local_cols + 1])
        - (padded[..., 4 : local_cols + 4] - padded[..., 0:local_cols])
    ) / 12.0
    tendency = (
        stream_part - fields[1] * (span_slope + metric_y * level_slope) - fields[2] * level_slope
    )
    tendency = tendency.at[2].add(BUOYANCY * fields[3])
    section = fields + SECTION_DT * tendency
    flux = (section[2] * section[3]).astype(jnp.bfloat16).reshape(-1)
    bin_index = joint_bin.reshape(-1)
    points = flux.shape[0]
    block_size = math.gcd(points, 32768)
    bin_iota = lax.iota(jnp.int32, BINS)[:, None]

    def accumulate(totals, pair):
        weights, indices = pair
        theta_hot = (bin_iota == (indices // BINS)[None, :]).astype(jnp.bfloat16)
        w_hot = jnp.where(
            bin_iota == (indices % BINS)[None, :], weights[None, :], jnp.zeros((), jnp.bfloat16)
        )
        product = lax.dot_general(
            theta_hot, w_hot, (((1,), (1,)), ((), ())), preferred_element_type=jnp.float32
        )
        return (totals + product, None)

    sums, _ = lax.scan(
        accumulate,
        jnp.zeros((BINS, BINS), jnp.float32),
        (flux.reshape(-1, block_size), bin_index.reshape(-1, block_size)),
    )
    scale = (BINS * BINS / (total_x * total_y * levels)) ** 0.5
    combined = lax.psum(sums, ("gx", "gy"))
    row_share = BINS // lax.axis_size("gx")
    col_share = BINS // lax.axis_size("gy")
    own_sums = lax.dynamic_slice(
        combined,
        (lax.axis_index("gx") * row_share, lax.axis_index("gy") * col_share),
        (row_share, col_share),
    )
    histogram = own_sums * scale
    return (tendency, histogram)


def solution(mesh):
    placed = (
        P(None, "gx", None, "gy"),
        P("gx", "gy"),
        P("gx", "gy"),
        P("gx"),
        P(),
        P("gx", None, "gy"),
    )
    return jax.shard_map(
        shards,
        mesh=mesh,
        in_specs=placed,
        out_specs=(P(None, "gx", None, "gy"), P("gx", "gy")),
        check_vma=False,
    )
```

profile of v0, /device:TPU:0, one launch (start us, length us, event | category | flops | bytes accessed | tf_op | source)
XLA Modules:
  0.0 2512.7 jit_solution(6658313686539628489)
XLA Ops:
  7.2 30.6 %copy.12 = f32[4,256,16,512]{1,0,3,2:T(4,128)} copy(f32[4,256,16,512]{3,2,1,0:T(8,128)} %param.10) | data formatting | bytes 67108864 | tf_op args[0]
  37.8 7.3 all-to-all-start
  45.1 78.6 %fusion.84 = f32[2048,2048,1]{1,0,2:T(8,128)} fusion(), kind=kLoop, calls=%fused_computation.48.clone.clone.1 | loop fusion | flops 146800640 | bytes 16777216 | tf_op jit(solution)/shard_map/ij,njc->nic/dot_general | solution.py:58
  123.6 645.5 %all-to-all-done = f32[4,256,8192]{1,0,2:T(4,128)} async-done(((f32[4,256,8192]{1,0,2:T(4,128)}), f32[4,256,8192]{1,0,2:T(4,128)}, u32[]{:S(2)}, u32[]{:S(2)}) %all-to-all-start) | async-done | bytes 33554464 | tf_op jit(solution)/shard_map/all_to_all | solution.py:72
  769.2 27.6 %copy.13 = f32[4,256,8192]{1,2,0:T(8,128)} copy(f32[4,256,8192]{1,0,2:T(4,128)} %all-to-all-done) | data formatting | bytes 67108864 | tf_op jit(solution)/shard_map/all_to_all | solution.py:72
  796.8 33.6 %copy.14 = f32[4,8,256,1024]{3,2,1,0:T(8,128)} copy(f32[4,8,256,1024]{2,3,1,0:T(8,128)} %bitcast.47) | data formatting | bytes 67108864 | tf_op jit(solution)/shard_map/all_to_all | solution.py:72
  830.4 221.7 %convolution_bitcast_fusion = f32[4,2048,1024]{2,1,0:T(8,128)} fusion(f32[4,2048,1024]{2,1,0:T(8,128)} %bitcast.48, f32[2048,2048,1]{1,0,2:T(8,128)} %fusion.84), kind=kOutput, calls=%fused_computation.45 | convolution fusion | flops 206158430208 | bytes 83886080 | tf_op jit(solution)/shard_map/ij,njc->nic/dot_general | solution.py:58
  1052.1 37.9 %copy.15 = f32[4,2048,1024]{2,0,1:T(4,128)} copy(f32[4,2048,1024]{2,1,0:T(8,128)} %convolution_bitcast_fusion) | data formatting | bytes 67108864 | tf_op jit(solution)/shard_map/ij,njc->nic/transpose | solution.py:58
  1090.0 7.1 all-to-all-start.1
  1097.2 10.8 fusion.75
  1107.9 6.4 copy.22
  1114.4 6.3 copy.21
  1124.8 8.1 broadcast_multiply_fusion.1
  1132.9 18.8 negate_bitcast_fusion
  1151.7 13.2 fusion.74
  1164.9 45.3 %fusion.73 = (f32[4,256,15,512]{3,2,1,0:T(8,128)}, f32[4,256,15,512]{3,2,1,0:T(8,128)}) fusion(f32[4,256,16,512]{3,2,1,0:T(8,128)} %param.10), kind=kLoop, calls=%fused_computation.101 | loop fusion | bytes 125829120 | tf_op jit(solution)/shard_map/slice | solution.py:38
  1210.2 9.4 reshape_reshape.4
  1219.6 5.9 copy.20
  1225.5 5.9 copy.18
  1231.4 592.0 %all-to-all-done.1 = f32[4,2048,1024]{2,0,1:T(4,128)} async-done(((f32[4,2048,1024]{2,0,1:T(4,128)}), f32[4,2048,1024]{2,0,1:T(4,128)}, u32[]{:S(2)}, u32[]{:S(2)}) %all-to-all-start.1) | async-done | bytes 33554464 | tf_op jit(solution)/shard_map/all_to_all | solution.py:74
  1823.3 31.8 %copy.16 = f32[4,256,8,1024]{3,2,1,0:T(8,128)} copy(f32[4,256,8,1024]{3,0,1,2:T(4,128)} %bitcast.8) | data formatting | bytes 67108864 | tf_op jit(solution)/shard_map/all_to_all | solution.py:74
  1855.2 35.7 %reshape.75 = f32[4,256,16,512]{3,2,1,0:T(8,128)} reshape(f32[4,256,8,1024]{3,2,1,0:T(8,128)} %copy.16) | data formatting | bytes 67108864 | tf_op jit(solution)/shard_map/reshape | solution.py:74
  1890.9 115.7 %fusion.21 = f32[4,256,16,512]{3,2,1,0:T(8,128)} fusion(f32[4,256,16,2]{3,2,1,0:T(8,128)} %copy.20, f32[4,256,16,512]{3,2,1,0:T(8,128)} %param.10, f32[4,256,16,2]{3,2,1,0:T(8,128)} %copy.18, f32[4,256,16,512]{3,2,1,0:T(8,128)} %reshape.75, f32[4,256,15,512]{3,2,1,0:T(8,128)} %get-tuple-element.131, f32[4,256,1,512]{3,2,1,0:T(1,128)} %get-tuple-element.133, ...), kind=kLoop, calls=%fused_computation.29 | loop fusion | flops 209715200 | bytes 210109504 | tf_op jit(solution)/shard_map/sub | solution.py:90
  2006.6 9.4 fusion.50
  2016.0 33.6 %multiply_add_fusion = f32[4,256,16,512]{3,2,1,0:T(8,128)} fusion(f32[4,256,16,512]{3,2,1,0:T(8,128)} %param.10, f32[4,256,16,512]{3,2,1,0:T(8,128)} %fusion.50), kind=kLoop, calls=%fused_computation.36 | loop fusion | flops 16777216 | bytes 100663296 | tf_op jit(solution)/shard_map/add | solution.py:93
  2049.5 8.8 fusion.49
  2058.3 7.4 convert_element_type.27
  2065.7 401.8 %while.15 = (s32[]{:T(128)}, f32[64,64]{1,0:T(8,128)S(1)}, s32[64,32768]{1,0:T(8,128)}, bf16[64,32768]{1,0:T(8,128)(2,1)}, s32[]{:T(128)}, /*index=5*/s32[]{:T(128)}) while((s32[]{:T(128)}, f32[64,64]{1,0:T(8,128)S(1)}, s32[64,32768]{1,0:T(8,128)}, bf16[64,32768]{1,0:T(8,128)(2,1)}, s32[]{:T(128)}, ...), condition=%wide.region_2.3_spmd.clone.clone, body=%wide.region_1.2_spmd.clone.clone.sunk | while | flops 275390464 | bytes 5341279 | solution.py:111
  2072.0 1.9 and_select_fusion.4
  2078.3 1.9 and_select_fusion.4
  2084.5 1.9 and_select_fusion.4
  2090.8 1.9 and_select_fusion.4
  2103.4 1.9 and_select_fusion.4
  2109.7 1.9 and_select_fusion.4
  2128.5 1.9 and_select_fusion.4
  2134.8 1.9 and_select_fusion.4
  2141.1 1.9 and_select_fusion.4
  2147.3 1.9 and_select_fusion.4
  2166.2 1.9 and_select_fusion.4
  2185.0 1.9 and_select_fusion.4
  2191.3 1.9 and_select_fusion.4
  2197.6 1.9 and_select_fusion.4
  2210.1 1.9 and_select_fusion.4
  2222.7 1.9 and_select_fusion.4
  2229.0 1.9 and_select_fusion.4
  2235.2 1.9 and_select_fusion.4
  2241.5 1.9 and_select_fusion.4
  2467.6 37.5 %psum.15 = f32[64,64]{1,0:T(8,128)S(1)} all-reduce(f32[64,64]{1,0:T(8,128)S(1)} %get-tuple-element.85), channel_id=1, replica_groups=mesh['gx'=8,'gy'=4] {'gx','gy'}, use_global_device_ids=true, to_apply=%region_3.4 | all-reduce | flops 4096 | bytes 32768 | tf_op jit(solution)/shard_map/psum | solution.py:117
  (324 shorter events, 367.3 us)
Async XLA Ops:
  37.8 731.4 %all-to-all-start = ((f32[4,256,8192]{1,0,2:T(4,128)}), f32[4,256,8192]{1,0,2:T(4,128)}, u32[]{:S(2)}, u32[]{:S(2)}) async-start(f32[4,256,8192]{1,0,2:T(4,128)} %bitcast.46), calls=%async_computation | async-start | bytes 67108864 | tf_op jit(solution)/shard_map/all_to_all | solution.py:72
  1090.0 733.3 %all-to-all-start.1 = ((f32[4,2048,1024]{2,0,1:T(4,128)}), f32[4,2048,1024]{2,0,1:T(4,128)}, u32[]{:S(2)}, u32[]{:S(2)}) async-start(f32[4,2048,1024]{2,0,1:T(4,128)} %copy.15), calls=%async_computation.1 | async-start | bytes 67108864 | tf_op jit(solution)/shard_map/all_to_all | solution.py:74
  1097.1 793.8 %all-reduce.2.cloned.1.call-start = ((), (), s32[]{:S(2)}) async-start(), calls=%async_computation.2 | async-start | bytes 262144 | tf_op jit(solution)/shard_map/psum | solution.py:19
  1107.9 16.8 copy-start
  1107.9 16.8 copy-start.1
  1114.3 105.3 %collective-permute-start.1 = (f32[4,256,16,2]{1,2,3,0:T(8,128)S(1)}, f32[4,256,16,2]{1,2,3,0:T(8,128)S(1)}, u32[]{:S(2)}, u32[]{:S(2)}) collective-permute-start(f32[4,256,16,2]{1,2,3,0:T(8,128)S(1)} %copy.22), channel_id=1, source_target_pairs={{0,1},{1,2},{2,3},{3,0},{4,5},{5,6},{6,7},{7,4},{8,9},{9,10},{10,1... | collective-permute-start | bytes 393224 | tf_op jit(solution)/shard_map/ppermute | solution.py:28
  1120.7 104.9 %collective-permute-start = (f32[4,256,16,2]{1,2,3,0:T(8,128)S(1)}, f32[4,256,16,2]{1,2,3,0:T(8,128)S(1)}, u32[]{:S(2)}, u32[]{:S(2)}) collective-permute-start(f32[4,256,16,2]{1,2,3,0:T(8,128)S(1)} %copy.21), channel_id=1, source_target_pairs={{1,0},{2,1},{3,2},{0,3},{5,4},{6,5},{7,6},{4,7},{9,8},{10,9},{11,1... | collective-permute-start | bytes 393224 | tf_op jit(solution)/shard_map/ppermute | solution.py:31
  1164.9 45.3 %copy-start.3 = (s32[256]{0:T(256)S(1)}, s32[256]{0:T(256)}, u32[]{:S(2)}) copy-start(s32[256]{0:T(256)} %param.13) | copy-start | bytes 3076
  2049.5 16.2 copy-start.2
Sparse Core Ops, SparseCore 0:
  1124.8 566.8 all-reduce.1
where the time goes:
time: 2530 us; the launch traced here: 2510 us
  waiting for transfers between devices  1240 us (49%)
  other arithmetic  476 us (19%)
  local copies, waits for them, and re-layouts  401 us (16%)
  matrix products  327 us (13%)
  blocking collectives  37.5 us (1%)
    all_to_all x1, waiting for transfers between devices, shards(): lax.all_to_all(flattened, 'gx', split_axis=2, concat_axis=1, tiled=True)  646 us
    all_to_all x1, waiting for transfers between devices, shards(): lax.all_to_all(derived, 'gx', split_axis=1, concat_axis=2, tiled=True)  592 us
    dot_general x1, matrix products, differentiate(): jnp.einsum('ij,njc->nic', matrix, pencil, precision=lax.Precision.HIGHEST)  222 us
    select_n x64, other arithmetic, accumulate(): theta_hot = (bin_iota == (indices // BINS)[None, :]).astype(jnp.bfloat16)  120 us
    sub x1, other arithmetic, shards(): stream_part - fields[1] * (span_slope + metric_y * level_slope)  116 us
    dot_general x64, matrix products, accumulate(): lax.dot_general(theta_hot, w_hot, (((1,), (1,)), ((), ())), preferred_ele...  105 us
    dynamic_slice x64, local copies, waits for them, and re-layouts, shards(): lax.scan(accumulate, jnp.zeros((BINS, BINS), jnp.float32), (flux.reshape(...  92.9 us
    dot_general x1, other arithmetic, differentiate(): jnp.einsum('ij,njc->nic', matrix, pencil, precision=lax.Precision.HIGHEST)  78.6 us
  transfers between devices with their start and end apart: 5, of which 2 were waited for; matrix products, arithmetic and copies ran while one was open for 11% of the time, Pallas kernels for 0%

commit v1 on v0

v1 whole, which is shorter than its diff:
```python
import functools
import math

import jax
import jax.numpy as jnp
import ml_dtypes
import numpy as np
from jax import lax
from jax.experimental import pallas as pl
from jax.experimental.pallas import tpu as pltpu
from jax.sharding import PartitionSpec as P

LEVELS = 384
BINS = 64


FRINGE_RATE = 0.5
BUOYANCY = 0.5
SECTION_DT = 0.25

FACTOR_TOLERANCE = 1e-9


def broadcast(block, axis, owner):
    block = jnp.where(lax.axis_index(axis) == owner, block, jnp.zeros_like(block))
    return lax.psum(block, axis)


def padded(rank):
    return -(-rank // 8) * 8


def derivative_block(count, size, distance):
    table = np.zeros(count)
    for k in range(1, count):
        value = math.pi / count * math.cos(math.pi * k / count) / math.sin(math.pi * k / count)
        table[k] = round(value * 2.0**45) / 2.0**45 * (1 if k % 2 == 0 else -1)
    offset = np.arange(size)[:, None] - np.arange(size)[None, :] + distance * size
    return table[offset % count]


def factored(block, tolerance):
    rest = block.copy()
    left, right = [], []
    while True:
        row, col = np.unravel_index(np.argmax(np.abs(rest)), rest.shape)
        pivot = rest[row, col]
        if abs(pivot) <= tolerance and left:
            break
        left.append(rest[:, col] / pivot)
        right.append(rest[row, :].copy())
        rest = rest - left[-1][:, None] * right[-1][None, :]
    return np.stack(left, 1), np.stack(right, 0)


def pieces(matrix):
    rest, parts = matrix, []
    for _ in range(3):
        parts.append(rest.astype(ml_dtypes.bfloat16))
        rest = rest - parts[-1].astype(np.float64)
    high, middle, low = parts
    return np.concatenate([high, middle, low, high, middle, high], 1)


def operators(count, size):
    ranks, encode, decode = [], [], [derivative_block(count, size, 0)]
    for distance in range(1, count // size):
        left, right = factored(derivative_block(count, size, distance), FACTOR_TOLERANCE)
        rank = left.shape[1]
        ranks.append(rank)
        decode.append(np.pad(left, ((0, 0), (0, padded(rank) - rank))))
        encode.append(np.pad(right, ((0, padded(rank) - rank), (0, 0))))
    return pieces(np.concatenate(encode, 0)), pieces(np.concatenate(decode, 1)), tuple(ranks)


def split(value):
    high = value.astype(jnp.bfloat16)
    rest = value - high.astype(jnp.float32)
    middle = rest.astype(jnp.bfloat16)
    low = (rest - middle.astype(jnp.float32)).astype(jnp.bfloat16)
    return jnp.concatenate([high, high, high, middle, middle, low], 0)


def encode_kernel(matrix_ref, f_ref, *out_refs, levels, ranks):
    size = f_ref.shape[1] // levels

    def at_pair(pair, carry):
        parts = [
            f_ref[0, pl.ds(2 * pair + k, size, stride=levels), :] for k in range(2)
        ]
        coded = jnp.dot(
            matrix_ref[...],
            split(jnp.concatenate(parts, 1)),
            preferred_element_type=jnp.float32,
        )
        start = 0
        for rank, out_ref in zip(ranks, out_refs):
            for k in range(2):
                out_ref[0, pl.ds(2 * pair + k, rank, stride=levels), :] = coded[
                    start : start + rank, 128 * k : 128 * k + 128
                ]
            start += padded(rank)
        return carry

    lax.fori_loop(0, levels // 2, at_pair, 0, unroll=2)


def encoded(matrix, fields, ranks):
    count, size, levels, cols = fields.shape
    width = 128
    return pl.pallas_call(
        functools.partial(encode_kernel, levels=levels, ranks=ranks),
        grid=(count, cols // width),
        in_specs=[
            pl.BlockSpec(matrix.shape, lambda n, j: (0, 0)),
            pl.BlockSpec((1, size * levels, width), lambda n, j: (n, 0, j)),
        ],
        out_specs=[
            pl.BlockSpec((1, rank * levels, width), lambda n, j: (n, 0, j)) for rank in ranks
        ],
        out_shape=[
            jax.ShapeDtypeStruct((count, rank * levels, cols), jnp.float32) for rank in ranks
        ],
        compiler_params=pltpu.CompilerParams(vmem_limit_bytes=48 << 20),
    )(matrix, fields.reshape(count, size * levels, cols))


def decode_kernel(matrix_ref, f_ref, *refs, levels, ranks):
    code_refs, out_ref, scratch = refs[: len(ranks)], refs[-2], refs[-1]
    size = f_ref.shape[1] // levels
    scratch[...] = jnp.zeros_like(scratch)

    def at_pair(pair, carry):
        for k in range(2):
            lanes = slice(128 * k, 128 * k + 128)
            start = size
            scratch[:size, lanes] = f_ref[0, pl.ds(2 * pair + k, size, stride=levels), :]
            for rank, code_ref in zip(ranks, code_refs):
                scratch[start : start + rank, lanes] = code_ref[
                    0, pl.ds(2 * pair + k, rank, stride=levels), :
                ]
                start += padded(rank)
        slope = jnp.dot(
            matrix_ref[...], split(scratch[...]), preferred_element_type=jnp.float32
        )
        for k in range(2):
            out_ref[0, pl.ds(2 * pair + k, size, stride=levels), :] = slope[
                :, 128 * k : 128 * k + 128
            ]
        return carry

    lax.fori_loop(0, levels // 2, at_pair, 0)


def decoded(matrix, fields, codes, ranks):
    count, size, levels, cols = fields.shape
    width = 128
    total = size + sum(padded(rank) for rank in ranks)
    return pl.pallas_call(
        functools.partial(decode_kernel, levels=levels, ranks=ranks),
        grid=(count, cols // width),
        in_specs=[
            pl.BlockSpec(matrix.shape, lambda n, j: (0, 0)),
            pl.BlockSpec((1, size * levels, width), lambda n, j: (n, 0, j)),
        ]
        + [pl.BlockSpec((1, rank * levels, width), lambda n, j: (n, 0, j)) for rank in ranks],
        out_specs=pl.BlockSpec((1, size * levels, width), lambda n, j: (n, 0, j)),
        out_shape=jax.ShapeDtypeStruct((count, size * levels, cols), jnp.float32),
        scratch_shapes=[pltpu.VMEM((total, 2 * width), jnp.float32)],
        compiler_params=pltpu.CompilerParams(vmem_limit_bytes=48 << 20),
    )(matrix, fields.reshape(count, size * levels, cols), *codes).reshape(fields.shape)


def tendency_kernel(mask_ref, f_ref, halo_ref, s_ref, plane_ref, sx_ref, sy_ref, jb_ref, out_ref, hist_ref, *, rows):
    step = pl.program_id(0)
    levels, cols = f_ref.shape[2], f_ref.shape[3]

    @pl.when(step == 0)
    def _():
        hist_ref[...] = jnp.zeros_like(hist_ref)

    level = lax.broadcasted_iota(jnp.int32, (levels, cols), 0)
    shape_factor = 1.0 - (level.astype(jnp.float32) + 0.5) / LEVELS
    first = level == 0
    last = level == levels - 1
    inv = jnp.where(first | last, 1.0, 0.5)
    lane16 = lax.broadcasted_iota(jnp.int32, (16, cols), 0).astype(jnp.float32)
    iotas = [(lane16 + 16.0 * j).astype(jnp.bfloat16) for j in range(BINS // 16)]
    one = jnp.ones((16, cols), jnp.bfloat16)
    zero = jnp.zeros((16, cols), jnp.bfloat16)

    def row(x, carry):
        f = [f_ref[n, x] for n in range(4)]
        u, v, w, th = f
        sx = jnp.broadcast_to(sx_ref[pl.ds(x, 1), :], (levels, cols))
        sy = jnp.broadcast_to(sy_ref[pl.ds(x, 1), :], (levels, cols))
        across = w - shape_factor * (u * sx + v * sy)
        across = across * inv
        v12 = v * (1.0 / 12.0)
        rate = FRINGE_RATE * mask_ref[step * rows + x].astype(jnp.float32)
        tend = []
        for n in range(4):
            g = f[n]
            if True:
                up = jnp.where(last, g, pltpu.roll(g, levels - 1, 0))
                down = jnp.where(first, g, pltpu.roll(g, 1, 0))
                p = jnp.concatenate([g, halo_ref[n, x]], axis=1)
                width = cols + 128
                d1 = (pltpu.roll(p, width - 1, 1) - pltpu.roll(p, 1, 1))[:, :cols]
                d2 = (pltpu.roll(p, width - 2, 1) - pltpu.roll(p, 2, 1))[:, :cols]
                t = rate * (plane_ref[n] - g) - u * s_ref[n, x] - v12 * (8.0 * d1 - d2) - across * (up - down)
                if n == 2:
                    t = t + BUOYANCY * th
            out_ref[n, x] = t
            tend.append(t)
        flux = ((w + SECTION_DT * tend[2]) * (th + SECTION_DT * tend[3])).astype(jnp.bfloat16).astype(jnp.float32)
        jb = jb_ref[x]
        tb = (jb >> 6).astype(jnp.float32)
        wb = (jb & (BINS - 1)).astype(jnp.float32)
        lhs, rhs = [], []
        for q in range(levels // 4):
            lq, rq = [], []
            for l in range(4 * q, 4 * q + 4):
                tl = jnp.broadcast_to(tb[l:l + 1], (16, cols)).astype(jnp.bfloat16)
                wl = jnp.broadcast_to(wb[l:l + 1], (16, cols)).astype(jnp.bfloat16)
                fl = jnp.broadcast_to(flux[l:l + 1], (16, cols)).astype(jnp.bfloat16)
                lq += [jnp.where(tl == i, one, zero) for i in iotas]
                rq += [jnp.where(wl == i, fl, zero) for i in iotas]
            lhs.append(jnp.concatenate(lq, 0))
            rhs.append(jnp.concatenate(rq, 0))
        lhs = jnp.concatenate(lhs, 1)
        rhs = jnp.concatenate(rhs, 1)
        hist_ref[...] += lax.dot_general(lhs, rhs, (((1,), (1,)), ((), ())), preferred_element_type=jnp.float32)
        return carry

    lax.fori_loop(0, rows, row, 0)


def tendency_call(mask, fields, halo, stream, plane, slope_x, slope_y, jbin, rows=8):
    _, R, L, C = fields.shape
    big = pl.BlockSpec((4, rows, L, C), lambda i, m: (0, i, 0, 0))
    row2 = pl.BlockSpec((rows, C), lambda i, m: (i, 0))
    return pl.pallas_call(
        functools.partial(tendency_kernel, rows=rows),
        grid_spec=pltpu.PrefetchScalarGridSpec(
            num_scalar_prefetch=1, grid=(R // rows,),
            in_specs=[big, pl.BlockSpec((4, rows, L, 128), lambda i, m: (0, i, 0, 0)), big,
                      pl.BlockSpec((4, L, C), lambda i, m: (0, 0, 0)), row2, row2,
                      pl.BlockSpec((rows, L, C), lambda i, m: (i, 0, 0))],
            out_specs=[big, pl.BlockSpec((256, 256), lambda i, m: (0, 0))]),
        out_shape=[jax.ShapeDtypeStruct(fields.shape, jnp.float32), jax.ShapeDtypeStruct((256, 256), jnp.float32)],
        compiler_params=pltpu.CompilerParams(vmem_limit_bytes=56 << 20),
    )(mask, fields, halo, stream, plane, slope_x, slope_y, jbin)


def shards(fields, slope_x, slope_y, fringe_mask, plane_x, joint_bin):
    field_count, local_rows, levels, local_cols = fields.shape
    span, stream = lax.axis_size("gy"), lax.axis_size("gx")
    total_x, total_y = local_rows * stream, local_cols * span
    encoder, decoder, ranks = operators(total_x, local_rows)
    codes = encoded(encoder, fields, ranks)
    codes = [
        lax.ppermute(code, "gx", [(i, (i + distance) % stream) for i in range(stream)])
        for distance, code in enumerate(codes, 1)
    ]
    forward = [(i, (i + 1) % span) for i in range(span)]
    backward = [(target, source) for source, target in forward]
    low = lax.ppermute(fields[..., -2:], "gy", forward)
    high = lax.ppermute(fields[..., :2], "gy", backward)
    halo = jnp.concatenate([high, jnp.zeros(fields.shape[:3] + (124,), jnp.float32), low], -1)
    owner = plane_x[0] // local_rows
    own_row = lax.dynamic_index_in_dim(fields, plane_x[0] % local_rows, 1, keepdims=False)
    plane = broadcast(own_row, "gx", owner)
    stream_slope = decoded(decoder, fields, codes, ranks)
    tendency, square = tendency_call(
        fringe_mask, fields, halo, stream_slope, plane, slope_x, slope_y, joint_bin
    )
    sums = sum(square[BINS * i : BINS * i + BINS, BINS * i : BINS * i + BINS] for i in range(4))
    scale = (BINS * BINS / (total_x * total_y * levels)) ** 0.5
    combined = lax.psum(sums, ("gx", "gy"))
    row_share, col_share = BINS // stream, BINS // span
    own_sums = lax.dynamic_slice(
        combined,
        (lax.axis_index("gx") * row_share, lax.axis_index("gy") * col_share),
        (row_share, col_share),
    )
    return tendency, own_sums * scale


def solution(mesh):
    placed = (
        P(None, "gx", None, "gy"),
        P("gx", "gy"),
        P("gx", "gy"),
        P("gx"),
        P(),
        P("gx", None, "gy"),
    )
    return jax.shard_map(
        shards,
        mesh=mesh,
        in_specs=placed,
        out_specs=(P(None, "gx", None, "gy"), P("gx", "gy")),
        check_vma=False,
    )
```

time: 2530 us -> 479 us (0.19)
  waiting for transfers between devices: 1240 us -> 86.3 us
  other arithmetic: 476 us -> 12.9 us
  local copies, waits for them, and re-layouts: 401 us -> 36 us
  matrix products: 327 us -> 0 us
  Pallas kernels: 0 us -> 278 us
    all_to_all x2 -> x0, waiting for transfers between devices: 1240 us -> none  [the longest x1 646 us: shards(): lax.all_to_all(flattened, 'gx', split_axis=2, concat_axis=1, tiled=True)]
    dot_general x65 -> x0, matrix products: 327 us -> none  [the longest x1 222 us: differentiate(): jnp.einsum('ij,njc->nic', matrix, pencil, precision=lax.Precision.HIGHEST)]
    pallas_call x0 -> x3, Pallas kernels: none -> 278 us  [the longest x1 163 us: tendency_call(): pl.pallas_call(functools.partial(tendency_kernel, rows=rows), grid_spec=p...]
    dot_general x65 -> x0, other arithmetic: 148 us -> none  [the longest x1 78.6 us: differentiate(): jnp.einsum('ij,njc->nic', matrix, pencil, precision=lax.Precision.HIGHEST)]
    select_n x129 -> x1, other arithmetic: 131 us -> 1.57 us  [broadcast(): jnp.where(lax.axis_index(axis) == owner, block, jnp.zeros_like(block))]
    sub x3 -> x0, other arithmetic: 117 us -> none  [the longest x1 116 us: shards(): stream_part - fields[1] * (span_slope + metric_y * level_slope)]
    all_to_all x3 -> x0, local copies, waits for them, and re-layouts: 93 us -> none  [the longest x2 61.2 us: shards(): lax.all_to_all(flattened, 'gx', split_axis=2, concat_axis=1, tiled=True)]
    dynamic_slice x64 -> x0, local copies, waits for them, and re-layouts: 92.9 us -> none  [shards(): lax.scan(accumulate, jnp.zeros((BINS, BINS), jnp.float32), (flux.reshape(...]
  transfers between devices with their start and end apart: 5 -> 10, of which waited for: 2 -> 3; matrix products, arithmetic and copies ran while one was open for 11% -> 10% of each run, Pallas kernels for 0% -> 16%
where the time goes in v1:
time: 479 us
  Pallas kernels  278 us (58%)
  waiting for transfers between devices  86.3 us (18%)
  blocking collectives  39.9 us (8%)
  local copies, waits for them, and re-layouts  36 us (8%)
  between operations  14.8 us (3%)
  other arithmetic  12.9 us (3%)
  starting transfers between devices  10.5 us (2%)
    pallas_call x1, Pallas kernels, tendency_call(): pl.pallas_call(functools.partial(tendency_kernel, rows=rows), grid_spec=p...  163 us
    ppermute x7, waiting for transfers between devices, shards(): lax.ppermute(code, 'gx', [(i, (i + distance) % stream) for i in range(str...  83.8 us
    pallas_call x1, Pallas kernels, decoded(): pl.pallas_call(functools.partial(decode_kernel, levels=levels, ranks=rank...  76.2 us
    psum x1, blocking collectives, shards(): combined = lax.psum(sums, ('gx', 'gy'))  39.9 us
    pallas_call x1, Pallas kernels, encoded(): pl.pallas_call(functools.partial(encode_kernel, levels=levels, ranks=rank...  38.6 us
    unnamed x12, local copies, waits for them, and re-layouts  13.5 us
    slice x1, local copies, waits for them, and re-layouts, shards(): high = lax.ppermute(fields[..., :2], 'gy', backward)  10.8 us
    concatenate x1, other arithmetic, shards(): jnp.concatenate([high, jnp.zeros(fields.shape[:3] + (124,), jnp.float32),...  9.72 us
  transfers between devices with their start and end apart: 10, of which 3 were waited for; matrix products, arithmetic and copies ran while one was open for 10% of the time, Pallas kernels for 16%

profile of v1, /device:TPU:0, one launch (start us, length us, event | category | flops | bytes accessed | tf_op | source)
XLA Modules:
  0.0 478.6 jit_solution(10687314560378331251)
XLA Ops:
  7.2 0.0 all-reduce.2.cloned.1.call-start
  7.2 0.0 copy-start.1
  7.2 0.9 copy-done.1
  8.1 38.6 %shard_map.95 = (f32[4,240,512]{2,1,0:T(8,128)}, f32[4,80,512]{2,1,0:T(8,128)}, f32[4,80,512]{2,1,0:T(8,128)S(1)}, f32[4,64,512]{2,1,0:T(8,128)}, f32[4,80,512]{...) custom-call(bf16[72,1536]{1,0:T(8,128)(2,1)S(1)} %copy-done.1, f32[4,4096,512]{2,1,0:T(8,128)} %bitcast.13), custom_call_target="tpu_custom_call" | custom-call | tf_op jit(solution)/shard_map/pallas_call | solution.py:111
  46.7 0.0 copy-start.2
  46.7 0.0 copy-start.3
  46.7 0.0 copy-start.4
  46.7 3.0 collective-permute-start.2
  49.8 3.1 collective-permute-start.8
  52.9 0.9 collective-permute-start.5
  53.8 1.6 collective-permute-start.3
  55.3 10.8 %fusion.1 = (f32[4,256,16,2]{3,2,1,0:T(8,128)}, f32[4,256,16,2]{3,2,1,0:T(8,128)}) fusion(f32[4,256,16,512]{3,2,1,0:T(8,128)} %f_ref.1), kind=kLoop, calls=%fused_computation.5 | loop fusion | bytes 524288 | tf_op jit(solution)/shard_map/slice | solution.py:269
  66.1 0.0 copy-done.2
  66.1 0.0 copy-done.3
  66.1 0.0 copy-done.4
  66.1 6.3 %copy.17 = f32[4,256,16,2]{1,2,3,0:T(8,128)S(1)} copy(f32[4,256,16,2]{3,2,1,0:T(8,128)} %get-tuple-element.21) | data formatting | bytes 262144
  72.4 0.0 collective-permute-start.1
  72.4 6.3 %copy.16 = f32[4,256,16,2]{1,2,3,0:T(8,128)S(1)} copy(f32[4,256,16,2]{3,2,1,0:T(8,128)} %get-tuple-element.20) | data formatting | bytes 262144
  78.7 0.0 collective-permute-done.1
  78.7 1.8 collective-permute-start
  80.5 2.5 collective-permute-done
  83.0 0.1 collective-permute-start.4
  83.1 78.4 %collective-permute-done.5.refs_3_ = f32[4,64,512]{2,1,0:T(8,128)} collective-permute-done((f32[4,64,512]{2,1,0:T(8,128)}, f32[4,64,512]{2,1,0:T(8,128)}, u32[]{:S(2)}, u32[]{:S(2)}) %collective-permute-start.5) | collective-permute-done | bytes 524320 | tf_op jit(solution)/shard_map/ppermute | solution.py:263
  161.5 0.0 collective-permute-start.6
  161.5 0.0 collective-permute-done.3.refs_1_
  161.5 0.0 collective-permute-start.7
  162.2 1.6 fusion
  163.8 0.0 all-reduce.2.cloned.1.call-update
  163.8 0.1 pad.1.clone
  163.9 5.9 %copy.13 = f32[4,256,16,2]{3,2,1,0:T(8,128)} copy(f32[4,256,16,2]{1,2,3,0:T(8,128)S(1)} %collective-permute-done) | data formatting | bytes 262144 | tf_op jit(solution)/shard_map/ppermute | solution.py:269
  169.8 5.8 %copy.14 = f32[4,256,16,2]{3,2,1,0:T(8,128)} copy(f32[4,256,16,2]{1,2,3,0:T(8,128)S(1)} %collective-permute-done.1) | data formatting | bytes 262144 | tf_op jit(solution)/shard_map/ppermute | solution.py:268
  175.6 0.0 copy-start
  175.6 9.7 %pad_maximum_fusion.halo_ref = f32[4,256,16,128]{3,2,1,0:T(8,128)} fusion(f32[4,256,16,2]{3,2,1,0:T(8,128)} %copy.14, f32[4,256,16,2]{3,2,1,0:T(8,128)} %copy.13, f32[128]{0:T(128)S(1)} %pad.1.clone), kind=kLoop, calls=%fused_computation | loop fusion | flops 4194304 | bytes 8651264 | tf_op jit(solution)/shard_map/concatenate | solution.py:270
  185.3 0.0 collective-permute-done.4.refs_2_
  185.3 0.0 collective-permute-done.6.refs_4_
  185.3 5.3 %collective-permute-done.7.refs_5_ = f32[4,80,512]{2,1,0:T(8,128)} collective-permute-done((f32[4,80,512]{2,1,0:T(8,128)}, f32[4,80,512]{2,1,0:T(8,128)}, u32[]{:S(2)}, u32[]{:S(2)}) %collective-permute-start.7) | collective-permute-done | bytes 655392 | tf_op jit(solution)/shard_map/ppermute | solution.py:263
  190.6 0.0 collective-permute-done.2.refs_0_
  190.6 0.0 collective-permute-done.8.refs_6_
  190.6 0.0 copy-done
  190.6 76.2 %shard_map.96 = f32[4,4096,512]{2,1,0:T(8,128)} custom-call(bf16[256,1968]{1,0:T(8,128)(2,1)S(1)} %copy-done, f32[4,4096,512]{2,1,0:T(8,128)} %bitcast.14, f32[4,240,512]{2,1,0:T(8,128)S(1)} %collective-permute-done.2.refs_0_, f32[4,80,512]{2,1,0:T(8,128)S(1)} %collective-permute-done.3.refs_1_, f32[4,80,512]{2,1,0:T(8,128)S(1)} %collective-permute-done.4.refs_2_, ...), custom_call_target="tpu_custom_call" | custom-call | tf_op jit(solution)/shard_map/pallas_call | solution.py:159
  266.9 0.0 all-reduce.2.cloned.1.call-done.plane_ref
  266.9 163.4 %shard_map.97 = (f32[4,256,16,512]{3,2,1,0:T(8,128)}, f32[256,256]{1,0:T(8,128)}) custom-call(s32[256]{0:T(256)} %mask_ref.1, f32[4,256,16,512]{3,2,1,0:T(8,128)} %f_ref.1, f32[4,256,16,128]{3,2,1,0:T(8,128)} %pad_maximum_fusion.halo_ref, f32[4,256,16,512]{3,2,1,0:T(8,128)} %bitcast.15, f32[4,16,512]{2,1,0:T(8,128)} %all-reduce.2.cloned.1.call-done.plane_ref, ...), custom_call_target="tpu_custom_call" | custom-call | tf_op jit(solution)/shard_map/pallas_call | solution.py:243
  430.3 0.9 slice_add_fusion
  431.2 39.9 %psum.15 = f32[64,64]{1,0:T(8,128)S(1)} all-reduce(f32[64,64]{1,0:T(8,128)S(1)} %slice_add_fusion), channel_id=1, replica_groups=mesh['gx'=8,'gy'=4] {'gx','gy'}, use_global_device_ids=true, to_apply=%region_1.2 | all-reduce | flops 4096 | bytes 32768 | tf_op jit(solution)/shard_map/psum | solution.py:280
  471.1 0.7 dynamic-slice_multiply_fusion
  (1 shorter events, 0.0 us)
Async XLA Ops:
  7.2 259.7 %all-reduce.2.cloned.1.call-start = ((), (), s32[]{:S(2)}) async-start(), calls=%async_computation | async-start | bytes 262144 | tf_op jit(solution)/shard_map/psum | solution.py:26
  7.2 0.9 copy-start.1
  46.7 19.4 %copy-start.2 = (f32[4,80,512]{2,1,0:T(8,128)}, f32[4,80,512]{2,1,0:T(8,128)S(1)}, u32[]{:S(2)}) copy-start(f32[4,80,512]{2,1,0:T(8,128)S(1)} %get-tuple-element.16) | copy-start | bytes 1966084
  46.7 19.4 %copy-start.3 = (f32[4,80,512]{2,1,0:T(8,128)}, f32[4,80,512]{2,1,0:T(8,128)S(1)}, u32[]{:S(2)}) copy-start(f32[4,80,512]{2,1,0:T(8,128)S(1)} %get-tuple-element.15) | copy-start | bytes 1966084
  46.7 19.4 %copy-start.4 = (f32[4,80,512]{2,1,0:T(8,128)}, f32[4,80,512]{2,1,0:T(8,128)S(1)}, u32[]{:S(2)}) copy-start(f32[4,80,512]{2,1,0:T(8,128)S(1)} %get-tuple-element.13) | copy-start | bytes 1966084
  46.7 143.9 %collective-permute-start.2 = (f32[4,240,512]{2,1,0:T(8,128)}, f32[4,240,512]{2,1,0:T(8,128)S(1)}, u32[]{:S(2)}, u32[]{:S(2)}) collective-permute-start(f32[4,240,512]{2,1,0:T(8,128)} %get-tuple-element.11), channel_id=1, source_target_pairs={{0,4},{4,8},{8,12},{12,16},{16,20},{20,24},{24,28},{28,0},{1,5},{5... | collective-permute-start | bytes 5898248 | tf_op jit(solution)/shard_map/ppermute | solution.py:263
  49.8 140.9 %collective-permute-start.8 = (f32[4,240,512]{2,1,0:T(8,128)}, f32[4,240,512]{2,1,0:T(8,128)}, u32[]{:S(2)}, u32[]{:S(2)}) collective-permute-start(f32[4,240,512]{2,1,0:T(8,128)} %get-tuple-element.17), channel_id=1, source_target_pairs={{0,28},{4,0},{8,4},{12,8},{16,12},{20,16},{24,20},{28,24},{1,29},{... | collective-permute-start | bytes 5898248 | tf_op jit(solution)/shard_map/ppermute | solution.py:263
  52.9 108.6 %collective-permute-start.5 = (f32[4,64,512]{2,1,0:T(8,128)}, f32[4,64,512]{2,1,0:T(8,128)}, u32[]{:S(2)}, u32[]{:S(2)}) collective-permute-start(f32[4,64,512]{2,1,0:T(8,128)} %get-tuple-element.14), channel_id=1, source_target_pairs={{0,16},{4,20},{8,24},{12,28},{16,0},{20,4},{24,8},{28,12},{1,17},{... | collective-permute-start | bytes 1572872 | tf_op jit(solution)/shard_map/ppermute | solution.py:263
  53.8 107.8 %collective-permute-start.3 = (f32[4,80,512]{2,1,0:T(8,128)}, f32[4,80,512]{2,1,0:T(8,128)S(1)}, u32[]{:S(2)}, u32[]{:S(2)}) collective-permute-start(f32[4,80,512]{2,1,0:T(8,128)} %get-tuple-element.12), channel_id=1, source_target_pairs={{0,8},{4,12},{8,16},{12,20},{16,24},{20,28},{24,0},{28,4},{1,9},{5... | collective-permute-start | bytes 1966088 | tf_op jit(solution)/shard_map/ppermute | solution.py:263
  72.4 6.3 %collective-permute-start.1 = (f32[4,256,16,2]{1,2,3,0:T(8,128)S(1)}, f32[4,256,16,2]{1,2,3,0:T(8,128)S(1)}, u32[]{:S(2)}, u32[]{:S(2)}) collective-permute-start(f32[4,256,16,2]{1,2,3,0:T(8,128)S(1)} %copy.17), channel_id=1, source_target_pairs={{0,1},{1,2},{2,3},{3,0},{4,5},{5,6},{6,7},{7,4},{8,9},{9,10},{10,1... | collective-permute-start | bytes 393224 | tf_op jit(solution)/shard_map/ppermute | solution.py:268
  78.7 4.3 collective-permute-start
  83.0 102.3 %collective-permute-start.4 = (f32[4,80,512]{2,1,0:T(8,128)}, f32[4,80,512]{2,1,0:T(8,128)S(1)}, u32[]{:S(2)}, u32[]{:S(2)}) collective-permute-start(f32[4,80,512]{2,1,0:T(8,128)} %copy-done.4), channel_id=1, source_target_pairs={{0,12},{4,16},{8,20},{12,24},{16,28},{20,0},{24,4},{28,8},{1,13},{... | collective-permute-start | bytes 1966088 | tf_op jit(solution)/shard_map/ppermute | solution.py:263
  161.5 23.8 %collective-permute-start.6 = (f32[4,80,512]{2,1,0:T(8,128)}, f32[4,80,512]{2,1,0:T(8,128)}, u32[]{:S(2)}, u32[]{:S(2)}) collective-permute-start(f32[4,80,512]{2,1,0:T(8,128)} %copy-done.3), channel_id=1, source_target_pairs={{0,20},{4,24},{8,28},{12,0},{16,4},{20,8},{24,12},{28,16},{1,21},{... | collective-permute-start | bytes 1966088 | tf_op jit(solution)/shard_map/ppermute | solution.py:263
  161.5 29.1 %collective-permute-start.7 = (f32[4,80,512]{2,1,0:T(8,128)}, f32[4,80,512]{2,1,0:T(8,128)}, u32[]{:S(2)}, u32[]{:S(2)}) collective-permute-start(f32[4,80,512]{2,1,0:T(8,128)} %copy-done.2), channel_id=1, source_target_pairs={{0,24},{4,28},{8,0},{12,4},{16,8},{20,12},{24,16},{28,20},{1,25},{... | collective-permute-start | bytes 1966088 | tf_op jit(solution)/shard_map/ppermute | solution.py:263
  175.6 15.1 %copy-start = (bf16[256,1968]{1,0:T(8,128)(2,1)S(1)}, bf16[256,1968]{1,0:T(8,128)(2,1)}, u32[]{:S(2)}) copy-start(bf16[256,1968]{1,0:T(8,128)(2,1)} %constant.55.clone.matrix_ref) | copy-start | bytes 3022852
Sparse Core Ops, SparseCore 0:
  163.9 80.2 all-reduce.1

commit v2 on v1

v2 whole, which is shorter than its diff:
```python
import functools
import math

import jax
import jax.numpy as jnp
import ml_dtypes
import numpy as np
from jax import lax
from jax.experimental import pallas as pl
from jax.experimental.pallas import tpu as pltpu
from jax.sharding import PartitionSpec as P

LEVELS = 384
BINS = 64


FRINGE_RATE = 0.5
BUOYANCY = 0.5
SECTION_DT = 0.25

FACTOR_TOLERANCE = 1e-9


def padded(rank):
    return -(-rank // 8) * 8


def derivative_block(count, size, distance):
    table = np.zeros(count)
    for k in range(1, count):
        value = math.pi / count * math.cos(math.pi * k / count) / math.sin(math.pi * k / count)
        table[k] = round(value * 2.0**45) / 2.0**45 * (1 if k % 2 == 0 else -1)
    offset = np.arange(size)[:, None] - np.arange(size)[None, :] + distance * size
    return table[offset % count]


def factored(block, tolerance):
    rest = block.copy()
    left, right = [], []
    while True:
        row, col = np.unravel_index(np.argmax(np.abs(rest)), rest.shape)
        pivot = rest[row, col]
        if abs(pivot) <= tolerance and left:
            break
        left.append(rest[:, col] / pivot)
        right.append(rest[row, :].copy())
        rest = rest - left[-1][:, None] * right[-1][None, :]
    return np.stack(left, 1), np.stack(right, 0)


def pieces(matrix):
    rest, parts = matrix, []
    for _ in range(3):
        parts.append(rest.astype(ml_dtypes.bfloat16))
        rest = rest - parts[-1].astype(np.float64)
    high, middle, low = parts
    return np.concatenate([high, middle, low, high, middle, high], 1)


def operators(count, size):
    ranks, encode, decode = [], [], [derivative_block(count, size, 0)]
    for distance in range(1, count // size):
        left, right = factored(derivative_block(count, size, distance), FACTOR_TOLERANCE)
        ranks.append(left.shape[1] + 1)
        spare = padded(ranks[-1]) - left.shape[1]
        decode.append(np.pad(left, ((0, 0), (0, spare))))
        encode.append(np.pad(right, ((0, spare), (0, 0))))
    return pieces(np.concatenate(encode, 0)), pieces(np.concatenate(decode, 1)), tuple(ranks)


def split(value):
    high = value.astype(jnp.bfloat16)
    rest = value - high.astype(jnp.float32)
    middle = rest.astype(jnp.bfloat16)
    low = (rest - middle.astype(jnp.float32)).astype(jnp.bfloat16)
    return jnp.concatenate([high, high, high, middle, middle, low], 0)


def encode_kernel(matrix_ref, f_ref, *out_refs, levels, ranks):
    size = f_ref.shape[1] // levels

    def at_pair(pair, carry):
        parts = [
            f_ref[0, pl.ds(2 * pair + k, size, stride=levels), :] for k in range(2)
        ]
        coded = jnp.dot(
            matrix_ref[...],
            split(jnp.concatenate(parts, 1)),
            preferred_element_type=jnp.float32,
        )
        start = 0
        for rank, out_ref in zip(ranks, out_refs):
            for k in range(2):
                out_ref[0, pl.ds(2 * pair + k, rank, stride=levels), :] = coded[
                    start : start + rank, 128 * k : 128 * k + 128
                ]
            start += padded(rank)
        return carry

    lax.fori_loop(0, levels // 2, at_pair, 0, unroll=4)


def encoded(matrix, fields, ranks, first, tiles):
    count, size, levels, _ = fields.shape
    width = 128
    cols = tiles * width
    return pl.pallas_call(
        functools.partial(encode_kernel, levels=levels, ranks=ranks),
        grid=(count, cols // width),
        in_specs=[
            pl.BlockSpec(matrix.shape, lambda n, j: (0, 0)),
            pl.BlockSpec((1, size * levels, width), lambda n, j: (n, 0, first + j)),
        ],
        out_specs=[
            pl.BlockSpec((1, rank * levels, width), lambda n, j: (n, 0, j)) for rank in ranks
        ],
        out_shape=[
            jax.ShapeDtypeStruct((count, rank * levels, cols), jnp.float32) for rank in ranks
        ],
        compiler_params=pltpu.CompilerParams(vmem_limit_bytes=48 << 20),
    )(matrix, fields.reshape(count, size * levels, fields.shape[3]))


def decode_kernel(matrix_ref, f_ref, *refs, levels, ranks):
    code_refs, out_ref, scratch = refs[: len(ranks)], refs[-2], refs[-1]
    size = f_ref.shape[1] // levels
    scratch[...] = jnp.zeros_like(scratch)
    stacks = scratch.shape[0]

    def at_pair(pair, stack):
        for k in range(2):
            lanes = slice(128 * k, 128 * k + 128)
            start = size
            stack[:size, lanes] = f_ref[0, pl.ds(2 * pair + k, size, stride=levels), :]
            for rank, code_ref in zip(ranks, code_refs):
                stack[start : start + rank, lanes] = code_ref[
                    0, pl.ds(2 * pair + k, rank, stride=levels), :
                ]
                start += padded(rank)
        slope = jnp.dot(
            matrix_ref[...], split(stack[...]), preferred_element_type=jnp.float32
        )
        for k in range(2):
            out_ref[0, pl.ds(2 * pair + k, size, stride=levels), :] = slope[
                :, 128 * k : 128 * k + 128
            ]

    def some_pairs(group, carry):
        for k in range(stacks):
            at_pair(group * stacks + k, scratch.at[k])
        return carry

    lax.fori_loop(0, levels // (2 * stacks), some_pairs, 0)


def decoded(matrix, fields, codes, ranks, first, tiles):
    count, size, levels, _ = fields.shape
    width = 128
    cols = tiles * width
    total = size + sum(padded(rank) for rank in ranks)
    return pl.pallas_call(
        functools.partial(decode_kernel, levels=levels, ranks=ranks),
        grid=(count, cols // width),
        in_specs=[
            pl.BlockSpec(matrix.shape, lambda n, j: (0, 0)),
            pl.BlockSpec((1, size * levels, width), lambda n, j: (n, 0, first + j)),
        ]
        + [pl.BlockSpec((1, rank * levels, width), lambda n, j: (n, 0, j)) for rank in ranks],
        out_specs=pl.BlockSpec((1, size * levels, width), lambda n, j: (n, 0, j)),
        out_shape=jax.ShapeDtypeStruct((count, size * levels, cols), jnp.float32),
        scratch_shapes=[pltpu.VMEM((4, total, 2 * width), jnp.float32)],
        compiler_params=pltpu.CompilerParams(vmem_limit_bytes=48 << 20),
    )(matrix, fields.reshape(count, size * levels, fields.shape[3]), *codes).reshape(
        count, size, levels, cols
    )


def tendency_kernel(mask_ref, f_ref, beside_ref, halo_ref, s_ref, plane_ref, sx_ref, sy_ref, jb_ref, square_ref, *refs, leading):
    out_ref, hist_ref = refs[-2:]
    step = pl.program_id(0)
    rows, levels, cols = f_ref.shape[1:]

    @pl.when(step == 0)
    def _():
        hist_ref[...] = square_ref[...]

    level = lax.broadcasted_iota(jnp.int32, (levels, cols), 0)
    shape_factor = 1.0 - (level.astype(jnp.float32) + 0.5) / LEVELS
    first = level == 0
    last = level == levels - 1
    inverse = jnp.where(first | last, 1.0, 0.5)
    inner_side = lax.broadcasted_iota(jnp.int32, (levels, 128), 1) < 64
    if not leading:
        inner_side = ~inner_side
    row16 = lax.broadcasted_iota(jnp.int32, (16, cols), 0).astype(jnp.float32)
    targets = [(row16 + 16.0 * j).astype(jnp.bfloat16) for j in range(BINS // 16)]
    one = jnp.ones((16, cols), jnp.bfloat16)
    zero = jnp.zeros((16, cols), jnp.bfloat16)

    def row(x, carry):
        f = [f_ref[n, x] for n in range(4)]
        u, v, w, theta = f
        sx = jnp.broadcast_to(sx_ref[pl.ds(x, 1), :], (levels, cols))
        sy = jnp.broadcast_to(sy_ref[pl.ds(x, 1), :], (levels, cols))
        across = (w - shape_factor * (u * sx + v * sy)) * inverse
        v12 = v * (1.0 / 12.0)
        rate = FRINGE_RATE * mask_ref[step * rows + x].astype(jnp.float32)
        tend = []
        for n in range(4):
            g = f[n]
            above = jnp.where(last, g, pltpu.roll(g, levels - 1, 0))
            below = jnp.where(first, g, pltpu.roll(g, 1, 0))
            edge = jnp.where(inner_side, beside_ref[n, x], halo_ref[n, x])
            wide = jnp.concatenate([g, edge], axis=1)
            width = cols + 128
            d1 = (pltpu.roll(wide, width - 1, 1) - pltpu.roll(wide, 1, 1))[:, :cols]
            d2 = (pltpu.roll(wide, width - 2, 1) - pltpu.roll(wide, 2, 1))[:, :cols]
            t = (
                rate * (plane_ref[n] - g)
                - u * s_ref[n, x]
                - v12 * (8.0 * d1 - d2)
                - across * (above - below)
            )
            if n == 2:
                t = t + BUOYANCY * theta
            out_ref[n, x] = t
            tend.append(t)
        flux = (w + SECTION_DT * tend[2]) * (theta + SECTION_DT * tend[3])
        flux = flux.astype(jnp.bfloat16).astype(jnp.float32)
        bins = jb_ref[x]
        theta_bin = (bins >> (BINS.bit_length() - 1)).astype(jnp.float32)
        w_bin = (bins & (BINS - 1)).astype(jnp.float32)
        lhs, rhs = [], []
        for start in range(0, levels, 4):
            lq, rq = [], []
            for k in range(start, start + 4):
                tr = jnp.broadcast_to(theta_bin[k : k + 1], (16, cols)).astype(jnp.bfloat16)
                wr = jnp.broadcast_to(w_bin[k : k + 1], (16, cols)).astype(jnp.bfloat16)
                fr = jnp.broadcast_to(flux[k : k + 1], (16, cols)).astype(jnp.bfloat16)
                lq += [jnp.where(tr == i, one, zero) for i in targets]
                rq += [jnp.where(wr == i, fr, zero) for i in targets]
            lhs.append(jnp.concatenate(lq, 0))
            rhs.append(jnp.concatenate(rq, 0))
        hist_ref[...] += lax.dot_general(
            jnp.concatenate(lhs, 1),
            jnp.concatenate(rhs, 1),
            (((1,), (1,)), ((), ())),
            preferred_element_type=jnp.float32,
        )
        return carry

    lax.fori_loop(0, rows, row, 0, unroll=8)


def tendency_half(mask, fields, halo, stream_slope, plane, slope_x, slope_y, jbin, square, previous):
    count, size, levels, total = fields.shape
    cols, rows = total // 2, 8
    leading = previous is None
    c = 0 if leading else 1
    tile = cols // 128 if leading else cols // 128 - 1
    big = pl.BlockSpec((count, rows, levels, cols), lambda i, m: (0, i, 0, c))
    plain = pl.BlockSpec((rows, cols), lambda i, m: (i, c))
    whole = pl.BlockSpec(square.shape, lambda i, m: (0, 0))
    return pl.pallas_call(
        functools.partial(tendency_kernel, leading=leading),
        grid_spec=pltpu.PrefetchScalarGridSpec(
            num_scalar_prefetch=1,
            grid=(size // rows,),
            in_specs=[
                big,
                pl.BlockSpec((count, rows, levels, 128), lambda i, m: (0, i, 0, tile)),
                pl.BlockSpec((count, rows, levels, 128), lambda i, m: (0, i, 0, 0)),
                pl.BlockSpec((count, rows, levels, cols), lambda i, m: (0, i, 0, 0)),
                pl.BlockSpec((count, levels, cols), lambda i, m: (0, 0, 0)),
                plain,
                plain,
                pl.BlockSpec((rows, levels, cols), lambda i, m: (i, 0, c)),
                whole,
            ]
            + ([] if leading else [pl.BlockSpec(memory_space=pl.ANY)]),
            out_specs=[big, whole],
        ),
        out_shape=[
            jax.ShapeDtypeStruct(fields.shape, jnp.float32),
            jax.ShapeDtypeStruct(square.shape, jnp.float32),
        ],
        input_output_aliases={} if leading else {10: 0},
        compiler_params=pltpu.CompilerParams(vmem_limit_bytes=48 << 20),
    )(mask, fields, fields, halo, stream_slope, plane, slope_x, slope_y, jbin, square,
      *([] if leading else [previous]))


def shards(fields, slope_x, slope_y, fringe_mask, plane_x, joint_bin):
    field_count, local_rows, levels, local_cols = fields.shape
    span, stream = lax.axis_size("gy"), lax.axis_size("gx")
    total_x, total_y = local_rows * stream, local_cols * span
    encoder, decoder, ranks = operators(total_x, local_rows)
    half = local_cols // 256

    def moved(code, distance):
        return lax.ppermute(code, "gx", [(i, (i + distance) % stream) for i in range(stream)])

    owner = plane_x[0] // local_rows
    own_row = lax.dynamic_index_in_dim(fields, plane_x[0] % local_rows, 1, keepdims=False)
    own_row = jnp.where(lax.axis_index("gx") == owner, own_row, jnp.zeros_like(own_row))
    picked = (lax.iota(jnp.int32, local_rows) == plane_x[0] % local_rows) & (
        lax.axis_index("gx") == owner
    )
    picked = picked.astype(jnp.bfloat16)
    nothing = jnp.zeros_like(picked)
    picked = jnp.concatenate([picked, nothing, nothing, picked, nothing, picked])
    last_rows = np.cumsum([0, *map(padded, ranks)])[:-1] + np.array(ranks) - 1
    plane_rows = np.isin(np.arange(encoder.shape[0]), last_rows)[:, None]
    encoder = jnp.where(plane_rows, picked[None, :], encoder)
    distances = range(1, stream)
    codes = encoded(encoder, fields, ranks, 0, half)
    codes = [moved(code, d) for code, d in zip(codes, distances)]
    later = encoded(encoder, fields, ranks, half, half)
    forward = [(i, (i + 1) % span) for i in range(span)]
    backward = [(target, source) for source, target in forward]
    low = lax.ppermute(fields[..., -2:], "gy", forward)
    high = lax.ppermute(fields[..., :2], "gy", backward)
    halo = jnp.concatenate([high, jnp.zeros(fields.shape[:3] + (124,), jnp.float32), low], -1)
    codes, later, halo = lax.optimization_barrier((codes, later, halo))
    held = [d for d in distances if 2 < d < stream - 2 and 2 * d != stream]
    later = [code if d in held else moved(code, d) for code, d in zip(later, distances)]
    stream_slope = decoded(decoder, fields, codes, ranks, 0, half)
    stream_slope, *rest = lax.optimization_barrier((stream_slope, *[later[d - 1] for d in held]))
    for code, d in zip(rest, held):
        later[d - 1] = moved(code, d)
    tendency = None
    square = jnp.zeros((4 * BINS, 4 * BINS), jnp.float32)
    for part in range(2):
        if part:
            later, tendency = lax.optimization_barrier((later, tendency))
            stream_slope = decoded(decoder, fields, later, ranks, half, half)
        arrived = later if part else codes
        plane = own_row[..., 128 * half * part : 128 * half * (part + 1)]
        for code, rank in zip(arrived, ranks):
            plane = plane + code[:, (rank - 1) * levels :]
        tendency, square = tendency_half(
            fringe_mask, fields, halo, stream_slope, plane, slope_x, slope_y, joint_bin, square, tendency
        )
    sums = sum(square[BINS * i : BINS * i + BINS, BINS * i : BINS * i + BINS] for i in range(4))
    scale = (BINS * BINS / (total_x * total_y * levels)) ** 0.5
    row_share, col_share = BINS // stream, BINS // span
    pieces_of = sums.reshape(stream, row_share, span, col_share).transpose(0, 2, 1, 3)
    pieces_of = pieces_of.reshape(stream * span, row_share * col_share)
    received = lax.all_to_all(pieces_of, ("gx", "gy"), split_axis=0, concat_axis=0, tiled=True)
    own_sums = received.sum(0).reshape(row_share, col_share)
    return tendency, own_sums * scale


def solution(mesh):
    placed = (
        P(None, "gx", None, "gy"),
        P("gx", "gy"),
        P("gx", "gy"),
        P("gx"),
        P(),
        P("gx", None, "gy"),
    )
    return jax.shard_map(
        shards,
        mesh=mesh,
        in_specs=placed,
        out_specs=(P(None, "gx", None, "gy"), P("gx", "gy")),
        check_vma=False,
    )
```

time: 479 us -> 353 us (0.74)
  Pallas kernels: 278 us -> 208 us
  waiting for transfers between devices: 86.3 us -> 19.1 us
  starting transfers between devices: 10.5 us -> 50.9 us
  blocking collectives: 39.9 us -> 13.2 us
  between operations: 14.8 us -> 1.51 us
  local copies, waits for them, and re-layouts: 36 us -> 44.4 us
    ppermute x7 -> x14, waiting for transfers between devices: 83.8 us -> 19.1 us  [moved(): lax.ppermute(code, 'gx', [(i, (i + distance) % stream) for i in range(str...]
    pallas_call x1 -> x2, Pallas kernels: 163 us -> 108 us  [tendency_half(): pl.pallas_call(functools.partial(tendency_kernel, leading=leading), grid_...]
    ppermute x7 -> x14, starting transfers between devices: 8.66 us -> 50.4 us  [moved(): lax.ppermute(code, 'gx', [(i, (i + distance) % stream) for i in range(str...]
    psum x1 -> x0, blocking collectives: 39.9 us -> none  [shards(): combined = lax.psum(sums, ('gx', 'gy'))]
    all_to_all x0 -> x1, blocking collectives: none -> 13.2 us  [shards(): lax.all_to_all(pieces_of, ('gx', 'gy'), split_axis=0, concat_axis=0, tile...]
    pallas_call x1 -> x2, Pallas kernels: 76.2 us -> 63.4 us  [decoded(): pl.pallas_call(functools.partial(decode_kernel, levels=levels, ranks=rank...]
    unnamed x12 -> x34, local copies, waits for them, and re-layouts: 13.5 us -> 19.2 us
    pallas_call x1 -> x2, Pallas kernels: 38.6 us -> 36.7 us  [encoded(): pl.pallas_call(functools.partial(encode_kernel, levels=levels, ranks=rank...]
  transfers between devices with their start and end apart: 10 -> 16, of which waited for: 3 -> 3; matrix products, arithmetic and copies ran while one was open for 10% -> 14% of each run, Pallas kernels for 16% -> 30%
where the time goes in v2:
time: 353 us; the launch traced here: 351 us
  Pallas kernels  208 us (59%)
  starting transfers between devices  50.9 us (14%)
  local copies, waits for them, and re-layouts  44.4 us (13%)
  waiting for transfers between devices  19.1 us (5%)
  other arithmetic  13.7 us (4%)
  blocking collectives  13.2 us (4%)
    pallas_call x2, Pallas kernels, tendency_half(): pl.pallas_call(functools.partial(tendency_kernel, leading=leading), grid_...  108 us
    pallas_call x2, Pallas kernels, decoded(): pl.pallas_call(functools.partial(decode_kernel, levels=levels, ranks=rank...  63.4 us
    ppermute x14, starting transfers between devices, moved(): lax.ppermute(code, 'gx', [(i, (i + distance) % stream) for i in range(str...  50.4 us
    pallas_call x2, Pallas kernels, encoded(): pl.pallas_call(functools.partial(encode_kernel, levels=levels, ranks=rank...  36.7 us
    unnamed x34, local copies, waits for them, and re-layouts  19.2 us
    ppermute x14, waiting for transfers between devices, moved(): lax.ppermute(code, 'gx', [(i, (i + distance) % stream) for i in range(str...  19.1 us
    all_to_all x1, blocking collectives, shards(): lax.all_to_all(pieces_of, ('gx', 'gy'), split_axis=0, concat_axis=0, tile...  13.2 us
    slice x1, local copies, waits for them, and re-layouts, shards(): high = lax.ppermute(fields[..., :2], 'gy', backward)  10.8 us
  transfers between devices with their start and end apart: 16, of which 3 were waited for; matrix products, arithmetic and copies ran while one was open for 14% of the time, Pallas kernels for 30%

profile of v2, /device:TPU:0, one launch (start us, length us, event | category | flops | bytes accessed | tf_op | source)
XLA Modules:
  0.0 351.0 jit_solution(5004987471366841405)
XLA Ops:
  1.4 0.2 dynamic-update-slice
  1.6 0.2 dynamic-update-slice.1
  1.8 0.2 dynamic-update-slice.2
  2.0 0.2 dynamic-update-slice.3
  2.3 0.2 dynamic-update-slice.4
  2.4 1.0 broadcast_select_fusion.matrix_ref
  3.5 18.4 %shard_map.104 = (f32[4,256,256]{2,1,0:T(8,128)}, f32[4,96,256]{2,1,0:T(8,128)}, f32[4,96,256]{2,1,0:T(8,128)}, f32[4,80,256]{2,1,0:T(8,128)}, f32[4,96,256]{2,1...) custom-call(bf16[72,1536]{1,0:T(8,128)(2,1)S(1)} %broadcast_select_fusion.matrix_ref, f32[4,4096,512]{2,1,0:T(8,128)} %bitcast.20), custom_call_target="tpu_custom_call" | custom-call | tf_op jit(solution)/shard_map/pallas_call | solution.py:107
  21.8 4.1 %collective-permute-start.3 = (f32[4,80,256]{2,1,0:T(8,128)}, f32[4,80,256]{2,1,0:T(8,128)}, u32[]{:S(2)}, u32[]{:S(2)}) collective-permute-start(f32[4,80,256]{2,1,0:T(8,128)} %get-tuple-element.49), channel_id=1, source_target_pairs={{0,16},{4,20},{8,24},{12,28},{16,0},{20,4},{24,8},{28,12},{1,17},{... | collective-permute-start | bytes 983048 | tf_op jit(solution)/shard_map/ppermute | solution.py:301
  25.9 1.6 collective-permute-start.1
  27.5 1.5 collective-permute-start
  29.0 3.2 collective-permute-start.6
  32.2 10.8 %fusion.13 = (f32[4,256,16,2]{3,2,1,0:T(8,128)}, f32[4,256,16,2]{3,2,1,0:T(8,128)}) fusion(f32[4,256,16,512]{3,2,1,0:T(8,128)} %beside_ref.3), kind=kLoop, calls=%fused_computation.22 | loop fusion | bytes 524288 | tf_op jit(solution)/shard_map/slice | solution.py:322
  43.0 6.3 %copy.22 = f32[4,256,16,2]{1,2,3,0:T(8,128)S(1)} copy(f32[4,256,16,2]{3,2,1,0:T(8,128)} %get-tuple-element.90) | data formatting | bytes 262144
  49.3 6.9 %copy.23 = f32[4,256,16,2]{1,2,3,0:T(8,128)} copy(f32[4,256,16,2]{3,2,1,0:T(8,128)} %get-tuple-element.91) | data formatting | bytes 262144
  56.2 0.6 copy-done.13
  56.9 0.5 collective-permute-start.8
  57.3 18.3 %shard_map.105 = (f32[4,256,256]{2,1,0:T(8,128)}, f32[4,96,256]{2,1,0:T(8,128)S(1)}, f32[4,96,256]{2,1,0:T(8,128)}, f32[4,80,256]{2,1,0:T(8,128)S(1)}, f32[4,96,...) custom-call(bf16[72,1536]{1,0:T(8,128)(2,1)S(1)} %broadcast_select_fusion.matrix_ref, ...), custom_call_target="tpu_custom_call" | custom-call | tf_op jit(solution)/shard_map/pallas_call | solution.py:107
  75.7 0.7 copy-done.11
  76.5 6.7 %copy.17 = f32[4,256,16,2]{3,2,1,0:T(8,128)} copy(f32[4,256,16,2]{1,2,3,0:T(8,128)} %copy-done.13) | data formatting | bytes 262144 | tf_op jit(solution)/shard_map/ppermute | solution.py:322
  83.2 6.6 %copy.18 = f32[4,256,16,2]{3,2,1,0:T(8,128)} copy(f32[4,256,16,2]{1,2,3,0:T(8,128)} %collective-permute-done.8) | data formatting | bytes 262144 | tf_op jit(solution)/shard_map/ppermute | solution.py:321
  89.8 3.8 %collective-permute-start.4 = (f32[4,96,256]{2,1,0:T(8,128)}, f32[4,96,256]{2,1,0:T(8,128)S(1)}, u32[]{:S(2)}, u32[]{:S(2)}) collective-permute-start(f32[4,96,256]{2,1,0:T(8,128)} %get-tuple-element.50), channel_id=1, source_target_pairs={{0,20},{4,24},{8,28},{12,0},{16,4},{20,8},{24,12},{28,16},{1,21},{... | collective-permute-start | bytes 1179656 | tf_op jit(solution)/shard_map/ppermute | solution.py:301
  93.6 0.5 collective-permute-start.5
  94.1 9.5 %pad_maximum_fusion.halo_ref = f32[4,256,16,128]{3,2,1,0:T(8,128)} fusion(f32[4,256,16,2]{3,2,1,0:T(8,128)} %copy.18, f32[4,256,16,2]{3,2,1,0:T(8,128)} %copy.17, f32[128]{0:T(128)S(1)} %pad.1.clone), kind=kLoop, calls=%fused_computation | loop fusion | flops 4194304 | bytes 8651264 | tf_op jit(solution)/shard_map/concatenate | solution.py:323
  103.7 7.4 %collective-permute-done.4.refs_4_ = f32[4,96,256]{2,1,0:T(8,128)S(1)} collective-permute-done((f32[4,96,256]{2,1,0:T(8,128)}, f32[4,96,256]{2,1,0:T(8,128)S(1)}, u32[]{:S(2)}, u32[]{:S(2)}) %collective-permute-start.4) | collective-permute-done | bytes 393248 | tf_op jit(solution)/shard_map/ppermute | solution.py:301
  111.1 2.6 collective-permute-done.5.refs_5_
  113.7 1.0 copy-done.3
  114.6 6.4 %collective-permute-start.9 = (f32[4,256,256]{2,1,0:T(8,128)}, f32[4,256,256]{2,1,0:T(8,128)}, u32[]{:S(2)}, u32[]{:S(2)}) collective-permute-start(f32[4,256,256]{2,1,0:T(8,128)} %get-tuple-element.61), channel_id=1, source_target_pairs={{0,4},{4,8},{8,12},{12,16},{16,20},{20,24},{24,28},{28,0},{1,5},{5... | collective-permute-start | bytes 3145736 | tf_op jit(solution)/shard_map/ppermute | solution.py:301
  121.1 2.0 collective-permute-start.15
  123.1 2.2 collective-permute-start.10
  125.3 1.2 collective-permute-start.12
  126.5 1.2 collective-permute-start.14
  127.7 1.2 copy-done.4
  128.9 31.7 %shard_map.106 = f32[4,4096,256]{2,1,0:T(8,128)} custom-call(bf16[256,1968]{1,0:T(8,128)(2,1)S(1)} %copy-done, f32[4,4096,512]{2,1,0:T(8,128)} %bitcast.22, f32[4,256,256]{2,1,0:T(8,128)S(1)} %collective-permute-done.refs_0_, f32[4,96,256]{2,1,0:T(8,128)S(1)} %collective-permute-done.1.refs_1_, f32[4,96,256]{2,1,0:T(8,128)} %collective-permute-done.2.refs_2_, ...), custom_call_target="tpu_custom_call" | custom-call | tf_op jit(solution)/shard_map/pallas_call | solution.py:161
  160.6 0.8 copy-done.5
  161.4 0.7 copy-done.6
  162.1 9.1 %collective-permute-done.12.refs_3_ = f32[4,80,256]{2,1,0:T(8,128)} collective-permute-done((f32[4,80,256]{2,1,0:T(8,128)S(1)}, f32[4,80,256]{2,1,0:T(8,128)}, u32[]{:S(2)}, u32[]{:S(2)}) %collective-permute-start.12) | collective-permute-done | bytes 327712 | tf_op jit(solution)/shard_map/ppermute | solution.py:301
  171.2 22.6 %collective-permute-start.11 = (f32[4,96,256]{2,1,0:T(8,128)}, f32[4,96,256]{2,1,0:T(8,128)}, u32[]{:S(2)}, u32[]{:S(2)}) collective-permute-start(f32[4,96,256]{2,1,0:T(8,128)} %get-tuple-element.72), channel_id=1, source_target_pairs={{0,12},{4,16},{8,20},{12,24},{16,28},{20,0},{24,4},{28,8},{1,13},{... | collective-permute-start | bytes 1179656 | tf_op jit(solution)/shard_map/ppermute | solution.py:301
  193.8 0.9 fusion
  194.7 1.0 fusion.12.plane_ref
  195.8 54.1 %shard_map.107 = (f32[4,256,16,512]{3,2,1,0:T(8,128)}, f32[256,256]{1,0:T(8,128)S(1)}) custom-call(s32[256]{0:T(256)S(1)} %copy-done.7, f32[4,256,16,512]{3,2,1,0:T(8,128)} %beside_ref.3, f32[4,256,16,512]{3,2,1,0:T(8,128)} %beside_ref.3, f32[4,256,16,128]{3,2,1,0:T(8,128)} %pad_maximum_fusion.halo_ref, f32[4,256,16,256]{3,2,1,0:T(8,128)} %bitcast.25, ...), custom_call_target="tpu_custom_call" | custom-call | tf_op jit(solution)/shard_map/pallas_call | solution.py:264
  250.0 1.1 fusion.6.plane_ref
  251.1 31.7 %shard_map.108 = f32[4,4096,256]{2,1,0:T(8,128)} custom-call(bf16[256,1968]{1,0:T(8,128)(2,1)S(1)} %copy-done, f32[4,4096,512]{2,1,0:T(8,128)} %bitcast.23, f32[4,256,256]{2,1,0:T(8,128)} %collective-permute-done.9.refs_0_, f32[4,96,256]{2,1,0:T(8,128)} %collective-permute-done.10.refs_1_, f32[4,96,256]{2,1,0:T(8,128)} %collective-permute-done.11.refs_2_, ...), custom_call_target="tpu_custom_call" | custom-call | tf_op jit(solution)/shard_map/pallas_call | solution.py:161
  282.8 54.1 %shard_map.109 = (f32[4,256,16,512]{3,2,1,0:T(8,128)}, f32[256,256]{1,0:T(8,128)S(1)}) custom-call(s32[256]{0:T(256)S(1)} %copy-done.7, f32[4,256,16,512]{3,2,1,0:T(8,128)} %beside_ref.3, f32[4,256,16,512]{3,2,1,0:T(8,128)} %beside_ref.3, f32[4,256,16,128]{3,2,1,0:T(8,128)} %pad_maximum_fusion.halo_ref, ...), custom_call_target="tpu_custom_call", output_to_operand_aliasing={{0}: (10, {})} | custom-call | tf_op jit(solution)/shard_map/pallas_call | solution.py:264
  336.8 0.1 slice_add_fusion.2
  336.9 0.1 reshape.33
  337.0 0.1 all_to_all.6
  337.2 13.2 %all_to_all.9 = f32[32,1,128]{2,1,0:T(1,128)S(1)} all-to-all(f32[32,1,128]{2,1,0:T(1,128)S(1)} %bitcast.27), channel_id=1, replica_groups=mesh['gx'=8,'gy'=4] {'gx','gy'}, dimensions={0} | all-to-all | bytes 32768 | tf_op jit(solution)/shard_map/all_to_all | solution.py:349
  350.4 0.7 mul.11
  (48 shorter events, 0.3 us)
Async XLA Ops:
  21.8 21.1 %copy-start.10 = (f32[4,96,256]{2,1,0:T(8,128)}, f32[4,96,256]{2,1,0:T(8,128)S(1)}, u32[]{:S(2)}) copy-start(f32[4,96,256]{2,1,0:T(8,128)S(1)} %get-tuple-element.51) | copy-start | bytes 1179652
  21.8 67.9 %collective-permute-start.3 = (f32[4,80,256]{2,1,0:T(8,128)}, f32[4,80,256]{2,1,0:T(8,128)}, u32[]{:S(2)}, u32[]{:S(2)}) collective-permute-start(f32[4,80,256]{2,1,0:T(8,128)} %get-tuple-element.49), channel_id=1, source_target_pairs={{0,16},{4,20},{8,24},{12,28},{16,0},{20,4},{24,8},{28,12},{1,17},{... | collective-permute-start | bytes 983048 | tf_op jit(solution)/shard_map/ppermute | solution.py:301
  25.9 67.7 %collective-permute-start.1 = (f32[4,96,256]{2,1,0:T(8,128)}, f32[4,96,256]{2,1,0:T(8,128)S(1)}, u32[]{:S(2)}, u32[]{:S(2)}) collective-permute-start(f32[4,96,256]{2,1,0:T(8,128)} %get-tuple-element.47), channel_id=1, source_target_pairs={{0,8},{4,12},{8,16},{12,20},{16,24},{20,28},{24,0},{28,4},{1,9},{5... | collective-permute-start | bytes 1179656 | tf_op jit(solution)/shard_map/ppermute | solution.py:301
  27.5 86.2 %collective-permute-start = (f32[4,256,256]{2,1,0:T(8,128)}, f32[4,256,256]{2,1,0:T(8,128)S(1)}, u32[]{:S(2)}, u32[]{:S(2)}) collective-permute-start(f32[4,256,256]{2,1,0:T(8,128)} %get-tuple-element.46), channel_id=1, source_target_pairs={{0,4},{4,8},{8,12},{12,16},{16,20},{20,24},{24,28},{28,0},{1,5},{5... | collective-permute-start | bytes 3145736 | tf_op jit(solution)/shard_map/ppermute | solution.py:301
  29.0 84.7 %collective-permute-start.6 = (f32[4,256,256]{2,1,0:T(8,128)}, f32[4,256,256]{2,1,0:T(8,128)S(1)}, u32[]{:S(2)}, u32[]{:S(2)}) collective-permute-start(f32[4,256,256]{2,1,0:T(8,128)} %get-tuple-element.52), channel_id=1, source_target_pairs={{0,28},{4,0},{8,4},{12,8},{16,12},{20,16},{24,20},{28,24},{1,29},{... | collective-permute-start | bytes 3145736 | tf_op jit(solution)/shard_map/ppermute | solution.py:301
  49.2 7.0 %collective-permute-start.7 = (f32[4,256,16,2]{1,2,3,0:T(8,128)S(1)}, f32[4,256,16,2]{1,2,3,0:T(8,128)S(1)}, u32[]{:S(2)}, u32[]{:S(2)}) collective-permute-start(f32[4,256,16,2]{1,2,3,0:T(8,128)S(1)} %copy.22), channel_id=1, source_target_pairs={{1,0},{2,1},{3,2},{0,3},{5,4},{6,5},{7,6},{4,7},{9,8},{10,9},{11,1... | collective-permute-start | bytes 393224 | tf_op jit(solution)/shard_map/ppermute | solution.py:322
  56.2 0.7 copy-start.13
  56.9 26.3 %collective-permute-start.8 = (f32[4,256,16,2]{1,2,3,0:T(8,128)}, f32[4,256,16,2]{1,2,3,0:T(8,128)}, u32[]{:S(2)}, u32[]{:S(2)}) collective-permute-start(f32[4,256,16,2]{1,2,3,0:T(8,128)} %copy.23), channel_id=1, source_target_pairs={{0,1},{1,2},{2,3},{3,0},{4,5},{5,6},{6,7},{7,4},{8,9},{9,10},{10,1... | collective-permute-start | bytes 393224 | tf_op jit(solution)/shard_map/ppermute | solution.py:321
  75.7 0.7 copy-start.11
  76.4 13.4 %copy-start.8 = (f32[4,96,256]{2,1,0:T(8,128)}, f32[4,96,256]{2,1,0:T(8,128)S(1)}, u32[]{:S(2)}) copy-start(f32[4,96,256]{2,1,0:T(8,128)S(1)} %get-tuple-element.62) | copy-start | bytes 1179652
  83.2 20.5 %collective-permute-start.2 = (f32[4,96,256]{2,1,0:T(8,128)}, f32[4,96,256]{2,1,0:T(8,128)}, u32[]{:S(2)}, u32[]{:S(2)}) collective-permute-start(f32[4,96,256]{2,1,0:T(8,128)} %get-tuple-element.48), channel_id=1, source_target_pairs={{0,12},{4,16},{8,20},{12,24},{16,28},{20,0},{24,4},{28,8},{1,13},{... | collective-permute-start | bytes 1179656 | tf_op jit(solution)/shard_map/ppermute | solution.py:301
  89.8 21.3 %collective-permute-start.4 = (f32[4,96,256]{2,1,0:T(8,128)}, f32[4,96,256]{2,1,0:T(8,128)S(1)}, u32[]{:S(2)}, u32[]{:S(2)}) collective-permute-start(f32[4,96,256]{2,1,0:T(8,128)} %get-tuple-element.50), channel_id=1, source_target_pairs={{0,20},{4,24},{8,28},{12,0},{16,4},{20,8},{24,12},{28,16},{1,21},{... | collective-permute-start | bytes 1179656 | tf_op jit(solution)/shard_map/ppermute | solution.py:301
  93.6 29.5 %copy-start.9 = (f32[4,96,256]{2,1,0:T(8,128)S(1)}, f32[4,96,256]{2,1,0:T(8,128)}, u32[]{:S(2)}) copy-start(f32[4,96,256]{2,1,0:T(8,128)} %copy-done.8) | copy-start | bytes 1179652
  93.6 31.7 %copy-start.12 = (f32[4,80,256]{2,1,0:T(8,128)S(1)}, f32[4,80,256]{2,1,0:T(8,128)}, u32[]{:S(2)}) copy-start(f32[4,80,256]{2,1,0:T(8,128)} %copy-done.11) | copy-start | bytes 983044
  93.6 34.1 %copy-start = (bf16[256,1968]{1,0:T(8,128)(2,1)S(1)}, bf16[256,1968]{1,0:T(8,128)(2,1)}, u32[]{:S(2)}) copy-start(bf16[256,1968]{1,0:T(8,128)(2,1)} %constant.56.clone.matrix_ref) | copy-start | bytes 3022852
  93.6 20.0 %collective-permute-start.5 = (f32[4,96,256]{2,1,0:T(8,128)}, f32[4,96,256]{2,1,0:T(8,128)S(1)}, u32[]{:S(2)}, u32[]{:S(2)}) collective-permute-start(f32[4,96,256]{2,1,0:T(8,128)} %copy-done.10), channel_id=1, source_target_pairs={{0,24},{4,28},{8,0},{12,4},{16,8},{20,12},{24,16},{28,20},{1,25},{... | collective-permute-start | bytes 1179656 | tf_op jit(solution)/shard_map/ppermute | solution.py:301
  113.7 1.0 copy-start.3
  114.6 81.1 %copy-start.7 = (s32[256]{0:T(256)S(1)}, s32[256]{0:T(256)}, u32[]{:S(2)}) copy-start(s32[256]{0:T(256)} %mask_ref.3) | copy-start | bytes 3076
  114.6 81.1 %copy-start.1 = (f32[256,512]{1,0:T(8,128)S(1)}, f32[256,512]{1,0:T(8,128)}, u32[]{:S(2)}) copy-start(f32[256,512]{1,0:T(8,128)} %sx_ref.3) | copy-start | bytes 1572868
  114.6 81.1 %copy-start.2 = (f32[256,512]{1,0:T(8,128)S(1)}, f32[256,512]{1,0:T(8,128)}, u32[]{:S(2)}) copy-start(f32[256,512]{1,0:T(8,128)} %sy_ref.3) | copy-start | bytes 1572868
  114.6 135.3 %collective-permute-start.9 = (f32[4,256,256]{2,1,0:T(8,128)}, f32[4,256,256]{2,1,0:T(8,128)}, u32[]{:S(2)}, u32[]{:S(2)}) collective-permute-start(f32[4,256,256]{2,1,0:T(8,128)} %get-tuple-element.61), channel_id=1, source_target_pairs={{0,4},{4,8},{8,12},{12,16},{16,20},{20,24},{24,28},{28,0},{1,5},{5... | collective-permute-start | bytes 3145736 | tf_op jit(solution)/shard_map/ppermute | solution.py:301
  121.1 128.9 %collective-permute-start.15 = (f32[4,256,256]{2,1,0:T(8,128)}, f32[4,256,256]{2,1,0:T(8,128)}, u32[]{:S(2)}, u32[]{:S(2)}) collective-permute-start(f32[4,256,256]{2,1,0:T(8,128)} %get-tuple-element.76), channel_id=1, source_target_pairs={{0,28},{4,0},{8,4},{12,8},{16,12},{20,16},{24,20},{28,24},{1,29},{... | collective-permute-start | bytes 3145736 | tf_op jit(solution)/shard_map/ppermute | solution.py:301
  123.1 70.7 %collective-permute-start.10 = (f32[4,96,256]{2,1,0:T(8,128)S(1)}, f32[4,96,256]{2,1,0:T(8,128)}, u32[]{:S(2)}, u32[]{:S(2)}) collective-permute-start(f32[4,96,256]{2,1,0:T(8,128)S(1)} %copy-done.9), channel_id=1, source_target_pairs={{0,8},{4,12},{8,16},{12,20},{16,24},{20,28},{24,0},{28,4},{1,9},{5... | collective-permute-start | bytes 1179656 | tf_op jit(solution)/shard_map/ppermute | solution.py:301
  125.3 45.9 %collective-permute-start.12 = (f32[4,80,256]{2,1,0:T(8,128)S(1)}, f32[4,80,256]{2,1,0:T(8,128)}, u32[]{:S(2)}, u32[]{:S(2)}) collective-permute-start(f32[4,80,256]{2,1,0:T(8,128)S(1)} %copy-done.12), channel_id=1, source_target_pairs={{0,16},{4,20},{8,24},{12,28},{16,0},{20,4},{24,8},{28,12},{1,17},{... | collective-permute-start | bytes 983048 | tf_op jit(solution)/shard_map/ppermute | solution.py:301
  126.5 123.5 %collective-permute-start.14 = (f32[4,96,256]{2,1,0:T(8,128)}, f32[4,96,256]{2,1,0:T(8,128)}, u32[]{:S(2)}, u32[]{:S(2)}) collective-permute-start(f32[4,96,256]{2,1,0:T(8,128)} %get-tuple-element.75), channel_id=1, source_target_pairs={{0,24},{4,28},{8,0},{12,4},{16,8},{20,12},{24,16},{28,20},{1,25},{... | collective-permute-start | bytes 1179656 | tf_op jit(solution)/shard_map/ppermute | solution.py:301
  127.7 1.2 copy-start.4
  160.6 0.8 copy-start.5
  161.4 0.7 copy-start.6
  171.2 78.7 %collective-permute-start.11 = (f32[4,96,256]{2,1,0:T(8,128)}, f32[4,96,256]{2,1,0:T(8,128)}, u32[]{:S(2)}, u32[]{:S(2)}) collective-permute-start(f32[4,96,256]{2,1,0:T(8,128)} %get-tuple-element.72), channel_id=1, source_target_pairs={{0,12},{4,16},{8,20},{12,24},{16,28},{20,0},{24,4},{28,8},{1,13},{... | collective-permute-start | bytes 1179656 | tf_op jit(solution)/shard_map/ppermute | solution.py:301
  193.8 56.2 %collective-permute-start.13 = (f32[4,96,256]{2,1,0:T(8,128)}, f32[4,96,256]{2,1,0:T(8,128)}, u32[]{:S(2)}, u32[]{:S(2)}) collective-permute-start(f32[4,96,256]{2,1,0:T(8,128)} %get-tuple-element.74), channel_id=1, source_target_pairs={{0,20},{4,24},{8,28},{12,0},{16,4},{20,8},{24,12},{28,16},{1,21},{... | collective-permute-start | bytes 1179656 | tf_op jit(solution)/shard_map/ppermute | solution.py:301

commit v3 on v2

--- a/solution.py
+++ b/solution.py
@@ -325,14 +325,12 @@
     held = [d for d in distances if 2 < d < stream - 2 and 2 * d != stream]
     later = [code if d in held else moved(code, d) for code, d in zip(later, distances)]
     stream_slope = decoded(decoder, fields, codes, ranks, 0, half)
-    stream_slope, *rest = lax.optimization_barrier((stream_slope, *[later[d - 1] for d in held]))
-    for code, d in zip(rest, held):
-        later[d - 1] = moved(code, d)
     tendency = None
     square = jnp.zeros((4 * BINS, 4 * BINS), jnp.float32)
     for part in range(2):
         if part:
             later, tendency = lax.optimization_barrier((later, tendency))
+            later = [moved(code, d) if d in held else code for code, d in zip(later, distances)]
             stream_slope = decoded(decoder, fields, later, ranks, half, half)
         arrived = later if part else codes
         plane = own_row[..., 128 * half * part : 128 * half * (part + 1)]

time: 353 us -> 348 us (0.986)
  starting transfers between devices: 50.9 us -> 32.9 us
  waiting for transfers between devices: 19.1 us -> 25.1 us
  blocking collectives: 13.2 us -> 17.1 us
    ppermute x14, starting transfers between devices: 50.4 us -> 32.4 us  [moved(): lax.ppermute(code, 'gx', [(i, (i + distance) % stream) for i in range(str...]
    ppermute x14, waiting for transfers between devices: 19.1 us -> 25.1 us  [moved(): lax.ppermute(code, 'gx', [(i, (i + distance) % stream) for i in range(str...]
    all_to_all x1, blocking collectives: 13.2 us -> 17.1 us  [shards(): lax.all_to_all(pieces_of, ('gx', 'gy'), split_axis=0, concat_axis=0, tile...]
    unnamed x34 -> x38, local copies, waits for them, and re-layouts: 19.2 us -> 22.2 us
where the time goes in v3:
time: 348 us; the launch traced here: 347 us
  Pallas kernels  209 us (60%)
  local copies, waits for them, and re-layouts  47.4 us (14%)
  starting transfers between devices  32.9 us (9%)
  waiting for transfers between devices  25.1 us (7%)
  blocking collectives  17.1 us (5%)
  other arithmetic  13.5 us (4%)
    pallas_call x2, Pallas kernels, tendency_half(): pl.pallas_call(functools.partial(tendency_kernel, leading=leading), grid_...  109 us
    pallas_call x2, Pallas kernels, decoded(): pl.pallas_call(functools.partial(decode_kernel, levels=levels, ranks=rank...  63.5 us
    pallas_call x2, Pallas kernels, encoded(): pl.pallas_call(functools.partial(encode_kernel, levels=levels, ranks=rank...  36.7 us
    ppermute x14, starting transfers between devices, moved(): lax.ppermute(code, 'gx', [(i, (i + distance) % stream) for i in range(str...  32.4 us
    ppermute x14, waiting for transfers between devices, moved(): lax.ppermute(code, 'gx', [(i, (i + distance) % stream) for i in range(str...  25.1 us
    unnamed x38, local copies, waits for them, and re-layouts  22.2 us
    all_to_all x1, blocking collectives, shards(): lax.all_to_all(pieces_of, ('gx', 'gy'), split_axis=0, concat_axis=0, tile...  17.1 us
    slice x1, local copies, waits for them, and re-layouts, shards(): high = lax.ppermute(fields[..., :2], 'gy', backward)  10.8 us
  transfers between devices with their start and end apart: 16, of which 3 were waited for; matrix products, arithmetic and copies ran while one was open for 14% of the time, Pallas kernels for 30%

profile of v3, /device:TPU:0, one launch (start us, length us, event | category | flops | bytes accessed | tf_op | source)
XLA Modules:
  0.0 346.9 jit_solution(15110201920932986168)
XLA Ops:
  1.4 0.2 dynamic-update-slice
  1.6 0.2 dynamic-update-slice.1
  1.8 0.2 dynamic-update-slice.2
  2.0 0.2 dynamic-update-slice.3
  2.3 0.2 dynamic-update-slice.4
  2.4 1.0 broadcast_select_fusion.matrix_ref
  3.5 18.4 %shard_map.104 = (f32[4,256,256]{2,1,0:T(8,128)}, f32[4,96,256]{2,1,0:T(8,128)S(1)}, f32[4,96,256]{2,1,0:T(8,128)}, f32[4,80,256]{2,1,0:T(8,128)}, f32[4,96,256]...) custom-call(bf16[72,1536]{1,0:T(8,128)(2,1)S(1)} %broadcast_select_fusion.matrix_ref, ...), custom_call_target="tpu_custom_call" | custom-call | tf_op jit(solution)/shard_map/pallas_call | solution.py:107
  21.8 4.1 %collective-permute-start.3 = (f32[4,80,256]{2,1,0:T(8,128)}, f32[4,80,256]{2,1,0:T(8,128)S(1)}, u32[]{:S(2)}, u32[]{:S(2)}) collective-permute-start(f32[4,80,256]{2,1,0:T(8,128)} %get-tuple-element.46), channel_id=1, source_target_pairs={{0,16},{4,20},{8,24},{12,28},{16,0},{20,4},{24,8},{28,12},{1,17},{... | collective-permute-start | bytes 983048 | tf_op jit(solution)/shard_map/ppermute | solution.py:301
  25.9 1.6 collective-permute-start.1
  27.5 1.5 collective-permute-start
  29.0 3.2 collective-permute-start.6
  32.2 10.8 %fusion.11 = (f32[4,256,16,2]{3,2,1,0:T(8,128)}, f32[4,256,16,2]{3,2,1,0:T(8,128)}) fusion(f32[4,256,16,512]{3,2,1,0:T(8,128)} %beside_ref.3), kind=kLoop, calls=%fused_computation.22 | loop fusion | bytes 524288 | tf_op jit(solution)/shard_map/slice | solution.py:322
  43.0 6.9 %copy.22 = f32[4,256,16,2]{1,2,3,0:T(8,128)} copy(f32[4,256,16,2]{3,2,1,0:T(8,128)} %get-tuple-element.84) | data formatting | bytes 262144
  49.9 6.9 %copy.23 = f32[4,256,16,2]{1,2,3,0:T(8,128)} copy(f32[4,256,16,2]{3,2,1,0:T(8,128)} %get-tuple-element.85) | data formatting | bytes 262144
  56.8 0.5 collective-permute-start.8
  57.3 18.4 %shard_map.105 = (f32[4,256,256]{2,1,0:T(8,128)}, f32[4,96,256]{2,1,0:T(8,128)}, f32[4,96,256]{2,1,0:T(8,128)S(1)}, f32[4,80,256]{2,1,0:T(8,128)S(1)}, f32[4,96,...) custom-call(bf16[72,1536]{1,0:T(8,128)(2,1)S(1)} %broadcast_select_fusion.matrix_ref, ...), custom_call_target="tpu_custom_call" | custom-call | tf_op jit(solution)/shard_map/pallas_call | solution.py:107
  75.7 0.8 copy-done.10
  76.5 0.7 copy-done.12
  77.2 0.7 copy-done.15
  78.0 6.7 %copy.17 = f32[4,256,16,2]{3,2,1,0:T(8,128)} copy(f32[4,256,16,2]{1,2,3,0:T(8,128)} %collective-permute-done.7) | data formatting | bytes 262144 | tf_op jit(solution)/shard_map/ppermute | solution.py:322
  84.7 6.6 %copy.18 = f32[4,256,16,2]{3,2,1,0:T(8,128)} copy(f32[4,256,16,2]{1,2,3,0:T(8,128)} %collective-permute-done.8) | data formatting | bytes 262144 | tf_op jit(solution)/shard_map/ppermute | solution.py:321
  91.3 0.7 copy-done.7
  92.0 3.8 %collective-permute-start.4 = (f32[4,96,256]{2,1,0:T(8,128)}, f32[4,96,256]{2,1,0:T(8,128)S(1)}, u32[]{:S(2)}, u32[]{:S(2)}) collective-permute-start(f32[4,96,256]{2,1,0:T(8,128)} %get-tuple-element.47), channel_id=1, source_target_pairs={{0,20},{4,24},{8,28},{12,0},{16,4},{20,8},{24,12},{28,16},{1,21},{... | collective-permute-start | bytes 1179656 | tf_op jit(solution)/shard_map/ppermute | solution.py:301
  95.8 0.4 collective-permute-start.5
  96.2 9.5 %pad_maximum_fusion.halo_ref = f32[4,256,16,128]{3,2,1,0:T(8,128)} fusion(f32[4,256,16,2]{3,2,1,0:T(8,128)} %copy.18, f32[4,256,16,2]{3,2,1,0:T(8,128)} %copy.17, f32[128]{0:T(128)S(1)} %pad.1.clone), kind=kLoop, calls=%fused_computation | loop fusion | flops 4194304 | bytes 8651264 | tf_op jit(solution)/shard_map/concatenate | solution.py:323
  105.8 7.4 %collective-permute-done.4.refs_4_ = f32[4,96,256]{2,1,0:T(8,128)S(1)} collective-permute-done((f32[4,96,256]{2,1,0:T(8,128)}, f32[4,96,256]{2,1,0:T(8,128)S(1)}, u32[]{:S(2)}, u32[]{:S(2)}) %collective-permute-start.4) | collective-permute-done | bytes 393248 | tf_op jit(solution)/shard_map/ppermute | solution.py:301
  113.2 0.7 copy-done.3
  114.0 1.0 collective-permute-done.5.refs_5_
  115.0 0.8 copy-done.5
  115.7 7.2 %collective-permute-start.9 = (f32[4,256,256]{2,1,0:T(8,128)}, f32[4,256,256]{2,1,0:T(8,128)}, u32[]{:S(2)}, u32[]{:S(2)}) collective-permute-start(f32[4,256,256]{2,1,0:T(8,128)} %get-tuple-element.58), channel_id=1, source_target_pairs={{0,4},{4,8},{8,12},{12,16},{16,20},{20,24},{24,28},{28,0},{1,5},{5... | collective-permute-start | bytes 3145736 | tf_op jit(solution)/shard_map/ppermute | solution.py:301
  123.0 2.8 collective-permute-start.13
  125.8 0.7 collective-permute-start.10
  126.5 3.1 collective-permute-start.12
  129.6 0.9 fusion
  130.6 1.0 copy-done.4
  131.6 1.0 copy-done.6
  132.6 1.0 copy-done.8
  133.5 31.8 %shard_map.106 = f32[4,4096,256]{2,1,0:T(8,128)} custom-call(bf16[256,1968]{1,0:T(8,128)(2,1)S(1)} %copy-done, f32[4,4096,512]{2,1,0:T(8,128)} %bitcast.22, f32[4,256,256]{2,1,0:T(8,128)S(1)} %collective-permute-done.refs_0_, f32[4,96,256]{2,1,0:T(8,128)S(1)} %collective-permute-done.1.refs_1_, f32[4,96,256]{2,1,0:T(8,128)} %collective-permute-done.2.refs_2_, ...), custom_call_target="tpu_custom_call" | custom-call | tf_op jit(solution)/shard_map/pallas_call | solution.py:161
  165.3 0.9 fusion.10.plane_ref
  166.3 54.7 %shard_map.107 = (f32[4,256,16,512]{3,2,1,0:T(8,128)}, f32[256,256]{1,0:T(8,128)S(1)}) custom-call(s32[256]{0:T(256)S(1)} %copy-done.9, f32[4,256,16,512]{3,2,1,0:T(8,128)} %beside_ref.3, f32[4,256,16,512]{3,2,1,0:T(8,128)} %beside_ref.3, f32[4,256,16,128]{3,2,1,0:T(8,128)} %pad_maximum_fusion.halo_ref, f32[4,256,16,256]{3,2,1,0:T(8,128)} %bitcast.25, ...), custom_call_target="tpu_custom_call" | custom-call | tf_op jit(solution)/shard_map/pallas_call | solution.py:264
  221.0 0.8 collective-permute-start.14
  221.8 3.1 collective-permute-start.15
  224.9 16.7 %collective-permute-done.14.refs_2_ = f32[4,96,256]{2,1,0:T(8,128)S(1)} collective-permute-done((f32[4,96,256]{2,1,0:T(8,128)S(1)}, f32[4,96,256]{2,1,0:T(8,128)S(1)}, u32[]{:S(2)}, u32[]{:S(2)}) %collective-permute-start.14) | collective-permute-done | bytes 393248 | tf_op jit(solution)/shard_map/ppermute | solution.py:301
  241.6 1.0 fusion.2.plane_ref
  242.5 31.8 %shard_map.108 = f32[4,4096,256]{2,1,0:T(8,128)} custom-call(bf16[256,1968]{1,0:T(8,128)(2,1)S(1)} %copy-done, f32[4,4096,512]{2,1,0:T(8,128)} %bitcast.23, f32[4,256,256]{2,1,0:T(8,128)} %collective-permute-done.9.refs_0_, f32[4,96,256]{2,1,0:T(8,128)} %collective-permute-done.10.refs_1_, f32[4,96,256]{2,1,0:T(8,128)S(1)} %collective-permute-done.14.refs_2_, ...), custom_call_target="tpu_custom_call" | custom-call | tf_op jit(solution)/shard_map/pallas_call | solution.py:161
  274.3 54.4 %shard_map.109 = (f32[4,256,16,512]{3,2,1,0:T(8,128)}, f32[256,256]{1,0:T(8,128)S(1)}) custom-call(s32[256]{0:T(256)S(1)} %copy-done.9, f32[4,256,16,512]{3,2,1,0:T(8,128)} %beside_ref.3, f32[4,256,16,512]{3,2,1,0:T(8,128)} %beside_ref.3, f32[4,256,16,128]{3,2,1,0:T(8,128)} %pad_maximum_fusion.halo_ref, ...), custom_call_target="tpu_custom_call", output_to_operand_aliasing={{0}: (10, {})} | custom-call | tf_op jit(solution)/shard_map/pallas_call | solution.py:264
  329.0 17.1 %all_to_all.9 = f32[32,1,128]{2,1,0:T(1,128)S(1)} all-to-all(f32[32,1,128]{2,1,0:T(1,128)S(1)} %bitcast.27), channel_id=1, replica_groups=mesh['gx'=8,'gy'=4] {'gx','gy'}, dimensions={0} | all-to-all | bytes 32768 | tf_op jit(solution)/shard_map/all_to_all | solution.py:347
  346.2 0.7 mul.11
  (52 shorter events, 0.6 us)
Async XLA Ops:
  21.8 21.2 %copy-start.14 = (f32[4,96,256]{2,1,0:T(8,128)}, f32[4,96,256]{2,1,0:T(8,128)S(1)}, u32[]{:S(2)}) copy-start(f32[4,96,256]{2,1,0:T(8,128)S(1)} %get-tuple-element.48) | copy-start | bytes 1179652
  21.8 69.4 %collective-permute-start.3 = (f32[4,80,256]{2,1,0:T(8,128)}, f32[4,80,256]{2,1,0:T(8,128)S(1)}, u32[]{:S(2)}, u32[]{:S(2)}) collective-permute-start(f32[4,80,256]{2,1,0:T(8,128)} %get-tuple-element.46), channel_id=1, source_target_pairs={{0,16},{4,20},{8,24},{12,28},{16,0},{20,4},{24,8},{28,12},{1,17},{... | collective-permute-start | bytes 983048 | tf_op jit(solution)/shard_map/ppermute | solution.py:301
  25.9 69.9 %collective-permute-start.1 = (f32[4,96,256]{2,1,0:T(8,128)S(1)}, f32[4,96,256]{2,1,0:T(8,128)S(1)}, u32[]{:S(2)}, u32[]{:S(2)}) collective-permute-start(f32[4,96,256]{2,1,0:T(8,128)S(1)} %get-tuple-element.44), channel_id=1, source_target_pairs={{0,8},{4,12},{8,16},{12,20},{16,24},{20,28},{24,0},{28,4},{1,9},{5... | collective-permute-start | bytes 1179656 | tf_op jit(solution)/shard_map/ppermute | solution.py:301
  27.5 88.3 %collective-permute-start = (f32[4,256,256]{2,1,0:T(8,128)}, f32[4,256,256]{2,1,0:T(8,128)S(1)}, u32[]{:S(2)}, u32[]{:S(2)}) collective-permute-start(f32[4,256,256]{2,1,0:T(8,128)} %get-tuple-element.43), channel_id=1, source_target_pairs={{0,4},{4,8},{8,12},{12,16},{16,20},{20,24},{24,28},{28,0},{1,5},{5... | collective-permute-start | bytes 3145736 | tf_op jit(solution)/shard_map/ppermute | solution.py:301
  29.0 86.8 %collective-permute-start.6 = (f32[4,256,256]{2,1,0:T(8,128)}, f32[4,256,256]{2,1,0:T(8,128)S(1)}, u32[]{:S(2)}, u32[]{:S(2)}) collective-permute-start(f32[4,256,256]{2,1,0:T(8,128)} %get-tuple-element.49), channel_id=1, source_target_pairs={{0,28},{4,0},{8,4},{12,8},{16,12},{20,16},{24,20},{28,24},{1,29},{... | collective-permute-start | bytes 3145736 | tf_op jit(solution)/shard_map/ppermute | solution.py:301
  49.9 6.9 %collective-permute-start.7 = (f32[4,256,16,2]{1,2,3,0:T(8,128)}, f32[4,256,16,2]{1,2,3,0:T(8,128)}, u32[]{:S(2)}, u32[]{:S(2)}) collective-permute-start(f32[4,256,16,2]{1,2,3,0:T(8,128)} %copy.22), channel_id=1, source_target_pairs={{1,0},{2,1},{3,2},{0,3},{5,4},{6,5},{7,6},{4,7},{9,8},{10,9},{11,1... | collective-permute-start | bytes 393224 | tf_op jit(solution)/shard_map/ppermute | solution.py:322
  56.8 27.9 %collective-permute-start.8 = (f32[4,256,16,2]{1,2,3,0:T(8,128)}, f32[4,256,16,2]{1,2,3,0:T(8,128)}, u32[]{:S(2)}, u32[]{:S(2)}) collective-permute-start(f32[4,256,16,2]{1,2,3,0:T(8,128)} %copy.23), channel_id=1, source_target_pairs={{0,1},{1,2},{2,3},{3,0},{4,5},{5,6},{6,7},{7,4},{8,9},{9,10},{10,1... | collective-permute-start | bytes 393224 | tf_op jit(solution)/shard_map/ppermute | solution.py:321
  75.7 0.8 copy-start.10
  76.5 0.7 copy-start.12
  77.2 0.7 copy-start.15
  84.7 21.1 %collective-permute-start.2 = (f32[4,96,256]{2,1,0:T(8,128)}, f32[4,96,256]{2,1,0:T(8,128)}, u32[]{:S(2)}, u32[]{:S(2)}) collective-permute-start(f32[4,96,256]{2,1,0:T(8,128)} %get-tuple-element.45), channel_id=1, source_target_pairs={{0,12},{4,16},{8,20},{12,24},{16,28},{20,0},{24,4},{28,8},{1,13},{... | collective-permute-start | bytes 1179656 | tf_op jit(solution)/shard_map/ppermute | solution.py:301
  91.3 0.7 copy-start.7
  92.0 21.2 %collective-permute-start.4 = (f32[4,96,256]{2,1,0:T(8,128)}, f32[4,96,256]{2,1,0:T(8,128)S(1)}, u32[]{:S(2)}, u32[]{:S(2)}) collective-permute-start(f32[4,96,256]{2,1,0:T(8,128)} %get-tuple-element.47), channel_id=1, source_target_pairs={{0,20},{4,24},{8,28},{12,0},{16,4},{20,8},{24,12},{28,16},{1,21},{... | collective-permute-start | bytes 1179656 | tf_op jit(solution)/shard_map/ppermute | solution.py:301
  95.8 34.7 %copy-start = (bf16[256,1968]{1,0:T(8,128)(2,1)S(1)}, bf16[256,1968]{1,0:T(8,128)(2,1)}, u32[]{:S(2)}) copy-start(bf16[256,1968]{1,0:T(8,128)(2,1)} %constant.56.clone.matrix_ref) | copy-start | bytes 3022852
  95.8 19.1 %collective-permute-start.5 = (f32[4,96,256]{2,1,0:T(8,128)}, f32[4,96,256]{2,1,0:T(8,128)S(1)}, u32[]{:S(2)}, u32[]{:S(2)}) collective-permute-start(f32[4,96,256]{2,1,0:T(8,128)} %copy-done.14), channel_id=1, source_target_pairs={{0,24},{4,28},{8,0},{12,4},{16,8},{20,12},{24,16},{28,20},{1,25},{... | collective-permute-start | bytes 1179656 | tf_op jit(solution)/shard_map/ppermute | solution.py:301
  113.2 0.7 copy-start.3
  115.0 0.8 copy-start.5
  115.7 105.2 %collective-permute-start.9 = (f32[4,256,256]{2,1,0:T(8,128)}, f32[4,256,256]{2,1,0:T(8,128)}, u32[]{:S(2)}, u32[]{:S(2)}) collective-permute-start(f32[4,256,256]{2,1,0:T(8,128)} %get-tuple-element.58), channel_id=1, source_target_pairs={{0,4},{4,8},{8,12},{12,16},{16,20},{20,24},{24,28},{28,0},{1,5},{5... | collective-permute-start | bytes 3145736 | tf_op jit(solution)/shard_map/ppermute | solution.py:301
  123.0 98.0 %collective-permute-start.13 = (f32[4,256,256]{2,1,0:T(8,128)}, f32[4,256,256]{2,1,0:T(8,128)}, u32[]{:S(2)}, u32[]{:S(2)}) collective-permute-start(f32[4,256,256]{2,1,0:T(8,128)} %get-tuple-element.64), channel_id=1, source_target_pairs={{0,28},{4,0},{8,4},{12,8},{16,12},{20,16},{24,20},{28,24},{1,29},{... | collective-permute-start | bytes 3145736 | tf_op jit(solution)/shard_map/ppermute | solution.py:301
  125.8 95.2 %collective-permute-start.10 = (f32[4,96,256]{2,1,0:T(8,128)}, f32[4,96,256]{2,1,0:T(8,128)}, u32[]{:S(2)}, u32[]{:S(2)}) collective-permute-start(f32[4,96,256]{2,1,0:T(8,128)} %get-tuple-element.59), channel_id=1, source_target_pairs={{0,8},{4,12},{8,16},{12,20},{16,24},{20,28},{24,0},{28,4},{1,9},{5... | collective-permute-start | bytes 1179656 | tf_op jit(solution)/shard_map/ppermute | solution.py:301
  126.5 94.4 %collective-permute-start.12 = (f32[4,96,256]{2,1,0:T(8,128)}, f32[4,96,256]{2,1,0:T(8,128)}, u32[]{:S(2)}, u32[]{:S(2)}) collective-permute-start(f32[4,96,256]{2,1,0:T(8,128)} %get-tuple-element.63), channel_id=1, source_target_pairs={{0,24},{4,28},{8,0},{12,4},{16,8},{20,12},{24,16},{28,20},{1,25},{... | collective-permute-start | bytes 1179656 | tf_op jit(solution)/shard_map/ppermute | solution.py:301
  129.6 91.3 %collective-permute-start.11 = (f32[4,80,256]{2,1,0:T(8,128)}, f32[4,80,256]{2,1,0:T(8,128)S(1)}, u32[]{:S(2)}, u32[]{:S(2)}) collective-permute-start(f32[4,80,256]{2,1,0:T(8,128)} %copy-done.15), channel_id=1, source_target_pairs={{0,16},{4,20},{8,24},{12,28},{16,0},{20,4},{24,8},{28,12},{1,17},{... | collective-permute-start | bytes 983048 | tf_op jit(solution)/shard_map/ppermute | solution.py:301
  130.6 1.0 copy-start.4
  131.6 1.0 copy-start.6
  132.6 1.0 copy-start.8
  133.5 32.7 %copy-start.1 = (f32[256,512]{1,0:T(8,128)S(1)}, f32[256,512]{1,0:T(8,128)}, u32[]{:S(2)}) copy-start(f32[256,512]{1,0:T(8,128)} %sx_ref.3) | copy-start | bytes 1572868
  133.5 32.7 %copy-start.2 = (f32[256,512]{1,0:T(8,128)S(1)}, f32[256,512]{1,0:T(8,128)}, u32[]{:S(2)}) copy-start(f32[256,512]{1,0:T(8,128)} %sy_ref.3) | copy-start | bytes 1572868
  133.5 32.7 %copy-start.9 = (s32[256]{0:T(256)S(1)}, s32[256]{0:T(256)}, u32[]{:S(2)}) copy-start(s32[256]{0:T(256)} %mask_ref.3) | copy-start | bytes 3076
  166.3 54.7 %copy-start.13 = (f32[4,96,256]{2,1,0:T(8,128)S(1)}, f32[4,96,256]{2,1,0:T(8,128)}, u32[]{:S(2)}) copy-start(f32[4,96,256]{2,1,0:T(8,128)} %copy-done.12) | copy-start | bytes 1179652
  166.3 55.5 %copy-start.11 = (f32[4,96,256]{2,1,0:T(8,128)S(1)}, f32[4,96,256]{2,1,0:T(8,128)}, u32[]{:S(2)}) copy-start(f32[4,96,256]{2,1,0:T(8,128)} %copy-done.10) | copy-start | bytes 1179652
  221.0 20.5 %collective-permute-start.14 = (f32[4,96,256]{2,1,0:T(8,128)S(1)}, f32[4,96,256]{2,1,0:T(8,128)S(1)}, u32[]{:S(2)}, u32[]{:S(2)}) collective-permute-start(f32[4,96,256]{2,1,0:T(8,128)S(1)} %copy-done.13), channel_id=1, source_target_pairs={{0,12},{4,16},{8,20},{12,24},{16,28},{20,0},{24,4},{28,8},{1,13},{... | collective-permute-start | bytes 1179656 | tf_op jit(solution)/shard_map/ppermute | solution.py:301
  221.8 19.8 %collective-permute-start.15 = (f32[4,96,256]{2,1,0:T(8,128)S(1)}, f32[4,96,256]{2,1,0:T(8,128)S(1)}, u32[]{:S(2)}, u32[]{:S(2)}) collective-permute-start(f32[4,96,256]{2,1,0:T(8,128)S(1)} %copy-done.11), channel_id=1, source_target_pairs={{0,20},{4,24},{8,28},{12,0},{16,4},{20,8},{24,12},{28,16},{1,21},{... | collective-permute-start | bytes 1179656 | tf_op jit(solution)/shard_map/ppermute | solution.py:301

commit v4 on v3

--- a/solution.py
+++ b/solution.py
@@ -168,7 +168,7 @@
         + [pl.BlockSpec((1, rank * levels, width), lambda n, j: (n, 0, j)) for rank in ranks],
         out_specs=pl.BlockSpec((1, size * levels, width), lambda n, j: (n, 0, j)),
         out_shape=jax.ShapeDtypeStruct((count, size * levels, cols), jnp.float32),
-        scratch_shapes=[pltpu.VMEM((4, total, 2 * width), jnp.float32)],
+        scratch_shapes=[pltpu.VMEM((8, total, 2 * width), jnp.float32)],
         compiler_params=pltpu.CompilerParams(vmem_limit_bytes=48 << 20),
     )(matrix, fields.reshape(count, size * levels, fields.shape[3]), *codes).reshape(
         count, size, levels, cols
@@ -249,12 +249,12 @@
         )
         return carry
 
-    lax.fori_loop(0, rows, row, 0, unroll=8)
+    lax.fori_loop(0, rows, row, 0, unroll=16)
 
 
 def tendency_half(mask, fields, halo, stream_slope, plane, slope_x, slope_y, jbin, square, previous):
     count, size, levels, total = fields.shape
-    cols, rows = total // 2, 8
+    cols, rows = total // 2, 16
     leading = previous is None
     c = 0 if leading else 1
     tile = cols // 128 if leading else cols // 128 - 1

time: 348 us -> 339 us (0.974)
  Pallas kernels: 209 us -> 201 us
    pallas_call x2, Pallas kernels: 109 us -> 104 us  [tendency_half(): pl.pallas_call(functools.partial(tendency_kernel, leading=leading), grid_...]
    pallas_call x2, Pallas kernels: 63.5 us -> 59.8 us  [decoded(): pl.pallas_call(functools.partial(decode_kernel, levels=levels, ranks=rank...]
  transfers between devices with their start and end apart: 16 -> 16, of which waited for: 3 -> 3; matrix products, arithmetic and copies ran while one was open for 14% -> 15% of each run, Pallas kernels for 30% -> 30%
where the time goes in v4:
time: 339 us; the launch traced here: 338 us
  Pallas kernels  201 us (59%)
  local copies, waits for them, and re-layouts  47.4 us (14%)
  starting transfers between devices  32.9 us (10%)
  waiting for transfers between devices  25.1 us (7%)
  blocking collectives  17.1 us (5%)
  other arithmetic  13.5 us (4%)
    pallas_call x2, Pallas kernels, tendency_half(): pl.pallas_call(functools.partial(tendency_kernel, leading=leading), grid_...  104 us
    pallas_call x2, Pallas kernels, decoded(): pl.pallas_call(functools.partial(decode_kernel, levels=levels, ranks=rank...  59.8 us
    pallas_call x2, Pallas kernels, encoded(): pl.pallas_call(functools.partial(encode_kernel, levels=levels, ranks=rank...  36.7 us
    ppermute x14, starting transfers between devices, moved(): lax.ppermute(code, 'gx', [(i, (i + distance) % stream) for i in range(str...  32.4 us
    ppermute x14, waiting for transfers between devices, moved(): lax.ppermute(code, 'gx', [(i, (i + distance) % stream) for i in range(str...  25.1 us
    unnamed x38, local copies, waits for them, and re-layouts  22.2 us
    all_to_all x1, blocking collectives, shards(): lax.all_to_all(pieces_of, ('gx', 'gy'), split_axis=0, concat_axis=0, tile...  17.1 us
    slice x1, local copies, waits for them, and re-layouts, shards(): high = lax.ppermute(fields[..., :2], 'gy', backward)  10.8 us
  transfers between devices with their start and end apart: 16, of which 3 were waited for; matrix products, arithmetic and copies ran while one was open for 15% of the time, Pallas kernels for 30%

profile of v4, /device:TPU:0, one launch (start us, length us, event | category | flops | bytes accessed | tf_op | source)
XLA Modules:
  0.0 338.4 jit_solution(12007283185592262753)
XLA Ops:
  1.4 0.2 dynamic-update-slice
  1.6 0.2 dynamic-update-slice.1
  1.8 0.2 dynamic-update-slice.2
  2.0 0.2 dynamic-update-slice.3
  2.3 0.2 dynamic-update-slice.4
  2.4 1.0 broadcast_select_fusion.matrix_ref
  3.5 18.4 %shard_map.104 = (f32[4,256,256]{2,1,0:T(8,128)}, f32[4,96,256]{2,1,0:T(8,128)S(1)}, f32[4,96,256]{2,1,0:T(8,128)}, f32[4,80,256]{2,1,0:T(8,128)}, f32[4,96,256]...) custom-call(bf16[72,1536]{1,0:T(8,128)(2,1)S(1)} %broadcast_select_fusion.matrix_ref, ...), custom_call_target="tpu_custom_call" | custom-call | tf_op jit(solution)/shard_map/pallas_call | solution.py:107
  21.8 4.1 %collective-permute-start.3 = (f32[4,80,256]{2,1,0:T(8,128)}, f32[4,80,256]{2,1,0:T(8,128)S(1)}, u32[]{:S(2)}, u32[]{:S(2)}) collective-permute-start(f32[4,80,256]{2,1,0:T(8,128)} %get-tuple-element.46), channel_id=1, source_target_pairs={{0,16},{4,20},{8,24},{12,28},{16,0},{20,4},{24,8},{28,12},{1,17},{... | collective-permute-start | bytes 983048 | tf_op jit(solution)/shard_map/ppermute | solution.py:301
  25.9 1.6 collective-permute-start.1
  27.5 1.5 collective-permute-start
  29.0 3.2 collective-permute-start.6
  32.2 10.8 %fusion.11 = (f32[4,256,16,2]{3,2,1,0:T(8,128)}, f32[4,256,16,2]{3,2,1,0:T(8,128)}) fusion(f32[4,256,16,512]{3,2,1,0:T(8,128)} %beside_ref.3), kind=kLoop, calls=%fused_computation.22 | loop fusion | bytes 524288 | tf_op jit(solution)/shard_map/slice | solution.py:322
  43.0 6.9 %copy.22 = f32[4,256,16,2]{1,2,3,0:T(8,128)} copy(f32[4,256,16,2]{3,2,1,0:T(8,128)} %get-tuple-element.84) | data formatting | bytes 262144
  49.9 6.9 %copy.23 = f32[4,256,16,2]{1,2,3,0:T(8,128)} copy(f32[4,256,16,2]{3,2,1,0:T(8,128)} %get-tuple-element.85) | data formatting | bytes 262144
  56.8 0.5 collective-permute-start.8
  57.3 18.4 %shard_map.105 = (f32[4,256,256]{2,1,0:T(8,128)}, f32[4,96,256]{2,1,0:T(8,128)}, f32[4,96,256]{2,1,0:T(8,128)S(1)}, f32[4,80,256]{2,1,0:T(8,128)S(1)}, f32[4,96,...) custom-call(bf16[72,1536]{1,0:T(8,128)(2,1)S(1)} %broadcast_select_fusion.matrix_ref, ...), custom_call_target="tpu_custom_call" | custom-call | tf_op jit(solution)/shard_map/pallas_call | solution.py:107
  75.7 0.8 copy-done.10
  76.5 0.7 copy-done.12
  77.2 0.7 copy-done.15
  78.0 6.7 %copy.17 = f32[4,256,16,2]{3,2,1,0:T(8,128)} copy(f32[4,256,16,2]{1,2,3,0:T(8,128)} %collective-permute-done.7) | data formatting | bytes 262144 | tf_op jit(solution)/shard_map/ppermute | solution.py:322
  84.7 6.6 %copy.18 = f32[4,256,16,2]{3,2,1,0:T(8,128)} copy(f32[4,256,16,2]{1,2,3,0:T(8,128)} %collective-permute-done.8) | data formatting | bytes 262144 | tf_op jit(solution)/shard_map/ppermute | solution.py:321
  91.3 0.7 copy-done.7
  92.0 3.8 %collective-permute-start.4 = (f32[4,96,256]{2,1,0:T(8,128)}, f32[4,96,256]{2,1,0:T(8,128)S(1)}, u32[]{:S(2)}, u32[]{:S(2)}) collective-permute-start(f32[4,96,256]{2,1,0:T(8,128)} %get-tuple-element.47), channel_id=1, source_target_pairs={{0,20},{4,24},{8,28},{12,0},{16,4},{20,8},{24,12},{28,16},{1,21},{... | collective-permute-start | bytes 1179656 | tf_op jit(solution)/shard_map/ppermute | solution.py:301
  95.8 0.4 collective-permute-start.5
  96.2 9.5 %pad_maximum_fusion.halo_ref = f32[4,256,16,128]{3,2,1,0:T(8,128)} fusion(f32[4,256,16,2]{3,2,1,0:T(8,128)} %copy.18, f32[4,256,16,2]{3,2,1,0:T(8,128)} %copy.17, f32[128]{0:T(128)S(1)} %pad.1.clone), kind=kLoop, calls=%fused_computation | loop fusion | flops 4194304 | bytes 8651264 | tf_op jit(solution)/shard_map/concatenate | solution.py:323
  105.8 7.4 %collective-permute-done.4.refs_4_ = f32[4,96,256]{2,1,0:T(8,128)S(1)} collective-permute-done((f32[4,96,256]{2,1,0:T(8,128)}, f32[4,96,256]{2,1,0:T(8,128)S(1)}, u32[]{:S(2)}, u32[]{:S(2)}) %collective-permute-start.4) | collective-permute-done | bytes 393248 | tf_op jit(solution)/shard_map/ppermute | solution.py:301
  113.2 0.7 copy-done.3
  114.0 1.0 collective-permute-done.5.refs_5_
  115.0 0.8 copy-done.5
  115.7 7.2 %collective-permute-start.9 = (f32[4,256,256]{2,1,0:T(8,128)}, f32[4,256,256]{2,1,0:T(8,128)}, u32[]{:S(2)}, u32[]{:S(2)}) collective-permute-start(f32[4,256,256]{2,1,0:T(8,128)} %get-tuple-element.58), channel_id=1, source_target_pairs={{0,4},{4,8},{8,12},{12,16},{16,20},{20,24},{24,28},{28,0},{1,5},{5... | collective-permute-start | bytes 3145736 | tf_op jit(solution)/shard_map/ppermute | solution.py:301
  123.0 2.8 collective-permute-start.13
  125.8 0.7 collective-permute-start.10
  126.5 3.1 collective-permute-start.12
  129.6 0.9 fusion
  130.6 1.0 copy-done.4
  131.6 1.0 copy-done.6
  132.6 1.0 copy-done.8
  133.5 29.8 %shard_map.106 = f32[4,4096,256]{2,1,0:T(8,128)} custom-call(bf16[256,1968]{1,0:T(8,128)(2,1)S(1)} %copy-done, f32[4,4096,512]{2,1,0:T(8,128)} %bitcast.22, f32[4,256,256]{2,1,0:T(8,128)S(1)} %collective-permute-done.refs_0_, f32[4,96,256]{2,1,0:T(8,128)S(1)} %collective-permute-done.1.refs_1_, f32[4,96,256]{2,1,0:T(8,128)} %collective-permute-done.2.refs_2_, ...), custom_call_target="tpu_custom_call" | custom-call | tf_op jit(solution)/shard_map/pallas_call | solution.py:161
  163.4 0.9 fusion.10.plane_ref
  164.3 52.3 %shard_map.107 = (f32[4,256,16,512]{3,2,1,0:T(8,128)}, f32[256,256]{1,0:T(8,128)S(1)}) custom-call(s32[256]{0:T(256)S(1)} %copy-done.9, f32[4,256,16,512]{3,2,1,0:T(8,128)} %beside_ref.3, f32[4,256,16,512]{3,2,1,0:T(8,128)} %beside_ref.3, f32[4,256,16,128]{3,2,1,0:T(8,128)} %pad_maximum_fusion.halo_ref, f32[4,256,16,256]{3,2,1,0:T(8,128)} %bitcast.25, ...), custom_call_target="tpu_custom_call" | custom-call | tf_op jit(solution)/shard_map/pallas_call | solution.py:264
  216.7 0.8 collective-permute-start.14
  217.4 3.1 collective-permute-start.15
  220.6 16.7 %collective-permute-done.14.refs_2_ = f32[4,96,256]{2,1,0:T(8,128)S(1)} collective-permute-done((f32[4,96,256]{2,1,0:T(8,128)S(1)}, f32[4,96,256]{2,1,0:T(8,128)S(1)}, u32[]{:S(2)}, u32[]{:S(2)}) %collective-permute-start.14) | collective-permute-done | bytes 393248 | tf_op jit(solution)/shard_map/ppermute | solution.py:301
  237.2 1.0 fusion.2.plane_ref
  238.2 29.9 %shard_map.108 = f32[4,4096,256]{2,1,0:T(8,128)} custom-call(bf16[256,1968]{1,0:T(8,128)(2,1)S(1)} %copy-done, f32[4,4096,512]{2,1,0:T(8,128)} %bitcast.23, f32[4,256,256]{2,1,0:T(8,128)} %collective-permute-done.9.refs_0_, f32[4,96,256]{2,1,0:T(8,128)} %collective-permute-done.10.refs_1_, f32[4,96,256]{2,1,0:T(8,128)S(1)} %collective-permute-done.14.refs_2_, ...), custom_call_target="tpu_custom_call" | custom-call | tf_op jit(solution)/shard_map/pallas_call | solution.py:161
  268.1 52.1 %shard_map.109 = (f32[4,256,16,512]{3,2,1,0:T(8,128)}, f32[256,256]{1,0:T(8,128)S(1)}) custom-call(s32[256]{0:T(256)S(1)} %copy-done.9, f32[4,256,16,512]{3,2,1,0:T(8,128)} %beside_ref.3, f32[4,256,16,512]{3,2,1,0:T(8,128)} %beside_ref.3, f32[4,256,16,128]{3,2,1,0:T(8,128)} %pad_maximum_fusion.halo_ref, ...), custom_call_target="tpu_custom_call", output_to_operand_aliasing={{0}: (10, {})} | custom-call | tf_op jit(solution)/shard_map/pallas_call | solution.py:264
  320.6 17.1 %all_to_all.9 = f32[32,1,128]{2,1,0:T(1,128)S(1)} all-to-all(f32[32,1,128]{2,1,0:T(1,128)S(1)} %bitcast.27), channel_id=1, replica_groups=mesh['gx'=8,'gy'=4] {'gx','gy'}, dimensions={0} | all-to-all | bytes 32768 | tf_op jit(solution)/shard_map/all_to_all | solution.py:347
  337.8 0.7 mul.11
  (52 shorter events, 0.6 us)
Async XLA Ops:
  21.8 21.2 %copy-start.14 = (f32[4,96,256]{2,1,0:T(8,128)}, f32[4,96,256]{2,1,0:T(8,128)S(1)}, u32[]{:S(2)}) copy-start(f32[4,96,256]{2,1,0:T(8,128)S(1)} %get-tuple-element.48) | copy-start | bytes 1179652
  21.8 69.4 %collective-permute-start.3 = (f32[4,80,256]{2,1,0:T(8,128)}, f32[4,80,256]{2,1,0:T(8,128)S(1)}, u32[]{:S(2)}, u32[]{:S(2)}) collective-permute-start(f32[4,80,256]{2,1,0:T(8,128)} %get-tuple-element.46), channel_id=1, source_target_pairs={{0,16},{4,20},{8,24},{12,28},{16,0},{20,4},{24,8},{28,12},{1,17},{... | collective-permute-start | bytes 983048 | tf_op jit(solution)/shard_map/ppermute | solution.py:301
  25.9 69.9 %collective-permute-start.1 = (f32[4,96,256]{2,1,0:T(8,128)S(1)}, f32[4,96,256]{2,1,0:T(8,128)S(1)}, u32[]{:S(2)}, u32[]{:S(2)}) collective-permute-start(f32[4,96,256]{2,1,0:T(8,128)S(1)} %get-tuple-element.44), channel_id=1, source_target_pairs={{0,8},{4,12},{8,16},{12,20},{16,24},{20,28},{24,0},{28,4},{1,9},{5... | collective-permute-start | bytes 1179656 | tf_op jit(solution)/shard_map/ppermute | solution.py:301
  27.5 88.3 %collective-permute-start = (f32[4,256,256]{2,1,0:T(8,128)}, f32[4,256,256]{2,1,0:T(8,128)S(1)}, u32[]{:S(2)}, u32[]{:S(2)}) collective-permute-start(f32[4,256,256]{2,1,0:T(8,128)} %get-tuple-element.43), channel_id=1, source_target_pairs={{0,4},{4,8},{8,12},{12,16},{16,20},{20,24},{24,28},{28,0},{1,5},{5... | collective-permute-start | bytes 3145736 | tf_op jit(solution)/shard_map/ppermute | solution.py:301
  29.0 86.8 %collective-permute-start.6 = (f32[4,256,256]{2,1,0:T(8,128)}, f32[4,256,256]{2,1,0:T(8,128)S(1)}, u32[]{:S(2)}, u32[]{:S(2)}) collective-permute-start(f32[4,256,256]{2,1,0:T(8,128)} %get-tuple-element.49), channel_id=1, source_target_pairs={{0,28},{4,0},{8,4},{12,8},{16,12},{20,16},{24,20},{28,24},{1,29},{... | collective-permute-start | bytes 3145736 | tf_op jit(solution)/shard_map/ppermute | solution.py:301
  49.9 6.9 %collective-permute-start.7 = (f32[4,256,16,2]{1,2,3,0:T(8,128)}, f32[4,256,16,2]{1,2,3,0:T(8,128)}, u32[]{:S(2)}, u32[]{:S(2)}) collective-permute-start(f32[4,256,16,2]{1,2,3,0:T(8,128)} %copy.22), channel_id=1, source_target_pairs={{1,0},{2,1},{3,2},{0,3},{5,4},{6,5},{7,6},{4,7},{9,8},{10,9},{11,1... | collective-permute-start | bytes 393224 | tf_op jit(solution)/shard_map/ppermute | solution.py:322
  56.8 27.9 %collective-permute-start.8 = (f32[4,256,16,2]{1,2,3,0:T(8,128)}, f32[4,256,16,2]{1,2,3,0:T(8,128)}, u32[]{:S(2)}, u32[]{:S(2)}) collective-permute-start(f32[4,256,16,2]{1,2,3,0:T(8,128)} %copy.23), channel_id=1, source_target_pairs={{0,1},{1,2},{2,3},{3,0},{4,5},{5,6},{6,7},{7,4},{8,9},{9,10},{10,1... | collective-permute-start | bytes 393224 | tf_op jit(solution)/shard_map/ppermute | solution.py:321
  75.7 0.8 copy-start.10
  76.5 0.7 copy-start.12
  77.2 0.7 copy-start.15
  84.7 21.1 %collective-permute-start.2 = (f32[4,96,256]{2,1,0:T(8,128)}, f32[4,96,256]{2,1,0:T(8,128)}, u32[]{:S(2)}, u32[]{:S(2)}) collective-permute-start(f32[4,96,256]{2,1,0:T(8,128)} %get-tuple-element.45), channel_id=1, source_target_pairs={{0,12},{4,16},{8,20},{12,24},{16,28},{20,0},{24,4},{28,8},{1,13},{... | collective-permute-start | bytes 1179656 | tf_op jit(solution)/shard_map/ppermute | solution.py:301
  91.3 0.7 copy-start.7
  92.0 21.2 %collective-permute-start.4 = (f32[4,96,256]{2,1,0:T(8,128)}, f32[4,96,256]{2,1,0:T(8,128)S(1)}, u32[]{:S(2)}, u32[]{:S(2)}) collective-permute-start(f32[4,96,256]{2,1,0:T(8,128)} %get-tuple-element.47), channel_id=1, source_target_pairs={{0,20},{4,24},{8,28},{12,0},{16,4},{20,8},{24,12},{28,16},{1,21},{... | collective-permute-start | bytes 1179656 | tf_op jit(solution)/shard_map/ppermute | solution.py:301
  95.8 34.7 %copy-start = (bf16[256,1968]{1,0:T(8,128)(2,1)S(1)}, bf16[256,1968]{1,0:T(8,128)(2,1)}, u32[]{:S(2)}) copy-start(bf16[256,1968]{1,0:T(8,128)(2,1)} %constant.56.clone.matrix_ref) | copy-start | bytes 3022852
  95.8 19.1 %collective-permute-start.5 = (f32[4,96,256]{2,1,0:T(8,128)}, f32[4,96,256]{2,1,0:T(8,128)S(1)}, u32[]{:S(2)}, u32[]{:S(2)}) collective-permute-start(f32[4,96,256]{2,1,0:T(8,128)} %copy-done.14), channel_id=1, source_target_pairs={{0,24},{4,28},{8,0},{12,4},{16,8},{20,12},{24,16},{28,20},{1,25},{... | collective-permute-start | bytes 1179656 | tf_op jit(solution)/shard_map/ppermute | solution.py:301
  113.2 0.7 copy-start.3
  115.0 0.8 copy-start.5
  115.7 100.9 %collective-permute-start.9 = (f32[4,256,256]{2,1,0:T(8,128)}, f32[4,256,256]{2,1,0:T(8,128)}, u32[]{:S(2)}, u32[]{:S(2)}) collective-permute-start(f32[4,256,256]{2,1,0:T(8,128)} %get-tuple-element.58), channel_id=1, source_target_pairs={{0,4},{4,8},{8,12},{12,16},{16,20},{20,24},{24,28},{28,0},{1,5},{5... | collective-permute-start | bytes 3145736 | tf_op jit(solution)/shard_map/ppermute | solution.py:301
  123.0 93.7 %collective-permute-start.13 = (f32[4,256,256]{2,1,0:T(8,128)}, f32[4,256,256]{2,1,0:T(8,128)}, u32[]{:S(2)}, u32[]{:S(2)}) collective-permute-start(f32[4,256,256]{2,1,0:T(8,128)} %get-tuple-element.64), channel_id=1, source_target_pairs={{0,28},{4,0},{8,4},{12,8},{16,12},{20,16},{24,20},{28,24},{1,29},{... | collective-permute-start | bytes 3145736 | tf_op jit(solution)/shard_map/ppermute | solution.py:301
  125.8 90.8 %collective-permute-start.10 = (f32[4,96,256]{2,1,0:T(8,128)}, f32[4,96,256]{2,1,0:T(8,128)}, u32[]{:S(2)}, u32[]{:S(2)}) collective-permute-start(f32[4,96,256]{2,1,0:T(8,128)} %get-tuple-element.59), channel_id=1, source_target_pairs={{0,8},{4,12},{8,16},{12,20},{16,24},{20,28},{24,0},{28,4},{1,9},{5... | collective-permute-start | bytes 1179656 | tf_op jit(solution)/shard_map/ppermute | solution.py:301
  126.5 90.1 %collective-permute-start.12 = (f32[4,96,256]{2,1,0:T(8,128)}, f32[4,96,256]{2,1,0:T(8,128)}, u32[]{:S(2)}, u32[]{:S(2)}) collective-permute-start(f32[4,96,256]{2,1,0:T(8,128)} %get-tuple-element.63), channel_id=1, source_target_pairs={{0,24},{4,28},{8,0},{12,4},{16,8},{20,12},{24,16},{28,20},{1,25},{... | collective-permute-start | bytes 1179656 | tf_op jit(solution)/shard_map/ppermute | solution.py:301
  129.6 87.0 %collective-permute-start.11 = (f32[4,80,256]{2,1,0:T(8,128)}, f32[4,80,256]{2,1,0:T(8,128)S(1)}, u32[]{:S(2)}, u32[]{:S(2)}) collective-permute-start(f32[4,80,256]{2,1,0:T(8,128)} %copy-done.15), channel_id=1, source_target_pairs={{0,16},{4,20},{8,24},{12,28},{16,0},{20,4},{24,8},{28,12},{1,17},{... | collective-permute-start | bytes 983048 | tf_op jit(solution)/shard_map/ppermute | solution.py:301
  130.6 1.0 copy-start.4
  131.6 1.0 copy-start.6
  132.6 1.0 copy-start.8
  133.5 30.8 %copy-start.1 = (f32[256,512]{1,0:T(8,128)S(1)}, f32[256,512]{1,0:T(8,128)}, u32[]{:S(2)}) copy-start(f32[256,512]{1,0:T(8,128)} %sx_ref.3) | copy-start | bytes 1572868
  133.5 30.8 %copy-start.2 = (f32[256,512]{1,0:T(8,128)S(1)}, f32[256,512]{1,0:T(8,128)}, u32[]{:S(2)}) copy-start(f32[256,512]{1,0:T(8,128)} %sy_ref.3) | copy-start | bytes 1572868
  133.5 30.8 %copy-start.9 = (s32[256]{0:T(256)S(1)}, s32[256]{0:T(256)}, u32[]{:S(2)}) copy-start(s32[256]{0:T(256)} %mask_ref.3) | copy-start | bytes 3076
  164.3 52.3 %copy-start.13 = (f32[4,96,256]{2,1,0:T(8,128)S(1)}, f32[4,96,256]{2,1,0:T(8,128)}, u32[]{:S(2)}) copy-start(f32[4,96,256]{2,1,0:T(8,128)} %copy-done.12) | copy-start | bytes 1179652
  164.3 53.1 %copy-start.11 = (f32[4,96,256]{2,1,0:T(8,128)S(1)}, f32[4,96,256]{2,1,0:T(8,128)}, u32[]{:S(2)}) copy-start(f32[4,96,256]{2,1,0:T(8,128)} %copy-done.10) | copy-start | bytes 1179652
  216.7 20.5 %collective-permute-start.14 = (f32[4,96,256]{2,1,0:T(8,128)S(1)}, f32[4,96,256]{2,1,0:T(8,128)S(1)}, u32[]{:S(2)}, u32[]{:S(2)}) collective-permute-start(f32[4,96,256]{2,1,0:T(8,128)S(1)} %copy-done.13), channel_id=1, source_target_pairs={{0,12},{4,16},{8,20},{12,24},{16,28},{20,0},{24,4},{28,8},{1,13},{... | collective-permute-start | bytes 1179656 | tf_op jit(solution)/shard_map/ppermute | solution.py:301
  217.4 19.8 %collective-permute-start.15 = (f32[4,96,256]{2,1,0:T(8,128)S(1)}, f32[4,96,256]{2,1,0:T(8,128)S(1)}, u32[]{:S(2)}, u32[]{:S(2)}) collective-permute-start(f32[4,96,256]{2,1,0:T(8,128)S(1)} %copy-done.11), channel_id=1, source_target_pairs={{0,20},{4,24},{8,28},{12,0},{16,4},{20,8},{24,12},{28,16},{1,21},{... | collective-permute-start | bytes 1179656 | tf_op jit(solution)/shard_map/ppermute | solution.py:301
